TPU v7x, 128 devices: a whole 4x4x4 slice. The times are simulated.
128 devices in a mesh: cell: 16 (over x, z_hi, core), tm: 8 (over y, z_lo).
Axes of the slice: x: 4, y: 4, z: 4 (z_hi: 2, z_lo: 2; z = z_hi * 2 + z_lo), core: 2. Of those that a mesh axis runs over, the one named last changes fastest.
Arguments:
- window: float32 [16384, 16384], P('cell', 'tm'), may hold values from -0.09375 to 0.09375
- range_test: float32 [16384, 256], P('tm'), may hold values from -0.046875 to 0.046875
- co_test: float32 [256, 16384], P(None, 'cell'), may hold values from -0.046875 to 0.046875
- core_left: float32 [512, 16384], P(None, 'cell'), may hold values from -0.046875 to 0.046875
- core_right: float32 [512, 16384], P(None, 'tm'), may hold values from -0.046875 to 0.046875
Outputs:
- range_basis: float32 [16384, 256], P('cell')
- co_basis: float32 [256, 16384], P(None, 'tm')
- core: float32 [256, 256], replicated
All inputs are finite; a program needn't handle non-finite values.
Results may differ from a plain program's by a relative error of at most 0.00023.
Values sent between devices are 32-bit elements; how exact they have to be, the bound alone decides.
A program may use at most 128 MiB of HBM per device.

v0:
```python
import math

import jax
import jax.numpy as jnp
from jax import lax
from jax.sharding import PartitionSpec as P


def inner_rows(left, right):
    return lax.dot_general(left, right, (((0,), (0,)), ((), ())), precision=lax.Precision.HIGHEST)


def inner_cols(left, right):
    return lax.dot_general(left, right, (((1,), (1,)), ((), ())), precision=lax.Precision.HIGHEST)


def product(left, right):
    return jnp.dot(left, right, precision=lax.Precision.HIGHEST, preferred_element_type=jnp.float32)


def per_device(window, range_test, co_test, core_left, core_right):
    rows_total = window.shape[0] * lax.axis_size("cell")
    cols_total = window.shape[1] * lax.axis_size("tm")
    range_term = product(window, range_test)
    co_term = product(co_test, window)
    left_window = product(core_left, window)
    core_term = inner_cols(left_window, core_right)
    sketch_z = lax.psum(core_term, ("cell", "tm"))
    range_full = lax.psum(range_term, "tm")
    co_full = lax.psum(co_term, "cell")
    gram_y = lax.psum(inner_rows(range_full, range_full) / rows_total, "cell")
    gram_w = lax.psum(inner_cols(co_full, co_full) / cols_total, "tm")
    lower_y = jnp.linalg.cholesky(gram_y)
    lower_w = jnp.linalg.cholesky(gram_w)
    range_basis = jax.scipy.linalg.solve_triangular(lower_y, range_full.T, lower=True).T
    co_basis = jax.scipy.linalg.solve_triangular(lower_w, co_full, lower=True)
    left_image = lax.psum(product(core_left, range_basis), "cell")
    right_image = lax.psum(inner_cols(core_right, co_basis), "tm")
    gram_left = inner_rows(left_image, left_image)
    gram_right = inner_rows(right_image, right_image)
    projected = inner_rows(left_image, sketch_z)
    left_solved = jax.scipy.linalg.cho_solve((jnp.linalg.cholesky(gram_left), True), projected)
    middle = product(left_solved, right_image)
    core = jax.scipy.linalg.cho_solve((jnp.linalg.cholesky(gram_right), True), middle.T).T
    core = core * math.sqrt(rows_total * cols_total)
    return (range_basis, co_basis, core)


def solution(mesh):
    return jax.shard_map(
        per_device,
        mesh=mesh,
        in_specs=(P("cell", "tm"), P("tm", None), P(None, "cell"), P(None, "cell"), P(None, "tm")),
        out_specs=(P("cell", None), P(None, "tm"), P()),
        check_vma=False,
    )
```

profile of v0, /device:TPU:1, one launch (start us, length us, event | category | flops | bytes accessed | tf_op | source)
XLA Modules:
  0.0 916.2 jit_solution(13198876106782574047)
XLA Ops:
  7.2 10.7 %fusion.50 = f32[1024,256]{1,0:T(8,128)} fusion(f32[1024,2048]{1,0:T(8,128)} %param.6, f32[2048,256]{1,0:T(8,128)} %param.7), kind=kOutput, calls=%fused_computation.123 | convolution fusion | flops 6442450944 | bytes 11534336 | tf_op jit(solution)/shard_map/dot_general | solution.py:18
  18.0 77.1 %all-reduce.9.cloned.1.call-done = f32[1024,256]{1,0:T(8,128)} async-done(((f32[1024,256]{1,0:T(8,128)}), f32[1024,256]{1,0:T(8,128)}) %all-reduce.9.cloned.1.call-update) | async-done | bytes 1048592 | tf_op jit(solution)/shard_map/psum | solution.py:29
  95.1 4.1 convolution_multiply_fusion.1
  99.2 10.7 %fusion.51 = f32[256,2048]{1,0:T(8,128)} fusion(f32[256,1024]{1,0:T(8,128)S(1)} %copy-done.12, f32[1024,2048]{1,0:T(8,128)} %param.6), kind=kOutput, calls=%fused_computation.124 | convolution fusion | flops 6442450944 | bytes 11534336 | tf_op jit(solution)/shard_map/dot_general | solution.py:18
  110.0 131.7 %all-reduce.11.cloned.1.call-done = f32[256,256]{0,1:T(8,128)} async-done(((f32[256,256]{0,1:T(8,128)}), f32[256,256]{0,1:T(8,128)}) %all-reduce.11.cloned.1.call-update) | async-done | bytes 262160 | tf_op jit(solution)/shard_map/psum | solution.py:31
  244.5 11.7 %cholesky.214 = f32[128,128]{1,0:T(8,128)S(1)} custom-call(f32[128,128]{1,0:T(8,128)S(1)} %cholesky.346), custom_call_target="Cholesky" | custom-call | tf_op jit(solution)/shard_map/jit(cholesky)/cholesky | solution.py:33
  256.2 9.8 %custom-call.37 = f32[1,128,128]{1,2,0:T(8,128)S(1)} custom-call(f32[1,128,128]{2,1,0:T(8,128)S(1)} %get-tuple-element.96), custom_call_target="InvertDiagBlocksLowerTriangular" | custom-call | tf_op jit(solution)/shard_map/jit(cholesky)/cholesky | solution.py:33
  268.2 11.7 %cholesky.231 = f32[128,128]{1,0:T(8,128)S(1)} custom-call(f32[128,128]{1,0:T(8,128)S(1)} %convolution_subtract_fusion.9), custom_call_target="Cholesky" | custom-call | tf_op jit(solution)/shard_map/jit(cholesky)/cholesky | solution.py:33
  283.0 4.1 while.4
  287.8 20.7 %custom-call.30 = f32[2,128,128]{1,2,0:T(8,128)S(1)} custom-call(f32[2,128,128]{2,1,0:T(8,128)} %copy-done.17), custom_call_target="InvertDiagBlocksLowerTriangular" | custom-call | tf_op jit(solution)/shard_map/jit(_solve_triangular)/triangular_solve | solution.py:35
  313.6 16.9 %fusion.54 = f32[512,2048]{1,0:T(8,128)S(1)} fusion(f32[512,1024]{1,0:T(8,128)S(1)} %copy-done, f32[1024,2048]{1,0:T(8,128)} %param.6), kind=kOutput, calls=%fused_computation.127 | convolution fusion | flops 12884901888 | bytes 14680064 | tf_op jit(solution)/shard_map/dot_general | solution.py:18
  330.6 7.9 fusion.55
  344.9 116.4 %all-reduce.19.cloned.1.call-done = (f32[256,2048]{1,0:T(8,128)}, f32[512,256]{0,1:T(8,128)}) async-done(((f32[256,2048]{1,0:T(8,128)}, f32[512,256]{0,1:T(8,128)}), (f32[256,2048]{1,0:T(8,128)}, f32[512,256]{0,1:T(8,128)})) %all-reduce.19.cloned.1.call-update) | async-done | bytes 2621456 | tf_op jit(solution)/shard_map/psum | solution.py:30
  463.2 11.7 %cholesky.316 = f32[128,128]{1,0:T(8,128)S(1)} custom-call(f32[128,128]{1,0:T(8,128)S(1)} %cholesky.355), custom_call_target="Cholesky" | custom-call | tf_op jit(solution)/shard_map/jit(cholesky)/cholesky | solution.py:42
  475.0 9.8 %custom-call.40 = f32[1,128,128]{1,2,0:T(8,128)S(1)} custom-call(f32[1,128,128]{2,1,0:T(8,128)S(1)} %get-tuple-element.88), custom_call_target="InvertDiagBlocksLowerTriangular" | custom-call | tf_op jit(solution)/shard_map/jit(cholesky)/cholesky | solution.py:42
  485.3 11.7 %cholesky.333 = f32[128,128]{1,0:T(8,128)S(1)} custom-call(f32[128,128]{1,0:T(8,128)S(1)} %convolution_subtract_fusion.6), custom_call_target="Cholesky" | custom-call | tf_op jit(solution)/shard_map/jit(cholesky)/cholesky | solution.py:42
  499.8 4.1 while.7
  503.9 19.7 %custom-call.33 = f32[2,128,128]{1,2,0:T(8,128)S(1)} custom-call(f32[2,128,128]{2,1,0:T(8,128)S(1)} %get-tuple-element.35), custom_call_target="InvertDiagBlocksLowerTriangular" | custom-call | tf_op jit(solution)/shard_map/jit(_cho_solve)/triangular_solve | solution.py:42
  523.6 4.8 convolution_multiply_fusion
  528.9 87.1 %all-reduce.17.cloned.1.call-done = f32[512,512]{1,0:T(8,128)} async-done(((f32[512,512]{1,0:T(8,128)}), f32[512,512]{1,0:T(8,128)}) %all-reduce.17.cloned.1.call-update) | async-done | bytes 1048592 | tf_op jit(solution)/shard_map/psum | solution.py:28
  619.5 66.9 %all-reduce.13.cloned.1.call-done = f32[256,256]{0,1:T(8,128)} async-done(((f32[256,256]{0,1:T(8,128)}), f32[256,256]{0,1:T(8,128)}) %all-reduce.13.cloned.1.call-update) | async-done | bytes 262160 | tf_op jit(solution)/shard_map/psum | solution.py:32
  688.6 11.7 %cholesky.248 = f32[128,128]{1,0:T(8,128)S(1)} custom-call(f32[128,128]{1,0:T(8,128)S(1)} %cholesky.349), custom_call_target="Cholesky" | custom-call | tf_op jit(solution)/shard_map/jit(cholesky)/cholesky | solution.py:34
  700.3 9.8 %custom-call.38 = f32[1,128,128]{1,2,0:T(8,128)S(1)} custom-call(f32[1,128,128]{2,1,0:T(8,128)S(1)} %get-tuple-element.92), custom_call_target="InvertDiagBlocksLowerTriangular" | custom-call | tf_op jit(solution)/shard_map/jit(cholesky)/cholesky | solution.py:34
  712.3 11.9 %cholesky.265 = f32[128,128]{1,0:T(8,128)S(1)} custom-call(f32[128,128]{1,0:T(8,128)S(1)} %convolution_subtract_fusion.8), custom_call_target="Cholesky" | custom-call | tf_op jit(solution)/shard_map/jit(cholesky)/cholesky | solution.py:34
  730.9 19.7 %custom-call.31 = f32[2,128,128]{1,2,0:T(8,128)S(1)} custom-call(f32[2,128,128]{2,1,0:T(8,128)S(1)} %get-tuple-element.19), custom_call_target="InvertDiagBlocksLowerTriangular" | custom-call | tf_op jit(solution)/shard_map/jit(_solve_triangular)/triangular_solve | solution.py:36
  758.0 4.5 convolution_bitcast_fusion.1
  763.7 73.2 %all-reduce.15.cloned.1.call-done = f32[512,256]{0,1:T(8,128)} async-done(((f32[512,256]{0,1:T(8,128)}), f32[512,256]{0,1:T(8,128)}) %all-reduce.15.cloned.1.call-update) | async-done | bytes 524304 | tf_op jit(solution)/shard_map/psum | solution.py:38
  841.3 11.9 %cholesky.282 = f32[128,128]{1,0:T(8,128)S(1)} custom-call(f32[128,128]{1,0:T(8,128)S(1)} %cholesky.352), custom_call_target="Cholesky" | custom-call | tf_op jit(solution)/shard_map/jit(cholesky)/cholesky | solution.py:44
  853.2 9.8 %custom-call.39 = f32[1,128,128]{1,2,0:T(8,128)S(1)} custom-call(f32[1,128,128]{2,1,0:T(8,128)S(1)} %get-tuple-element.84), custom_call_target="InvertDiagBlocksLowerTriangular" | custom-call | tf_op jit(solution)/shard_map/jit(cholesky)/cholesky | solution.py:44
  865.2 11.7 %cholesky.299 = f32[128,128]{1,0:T(8,128)S(1)} custom-call(f32[128,128]{1,0:T(8,128)S(1)} %convolution_subtract_fusion.7), custom_call_target="Cholesky" | custom-call | tf_op jit(solution)/shard_map/jit(cholesky)/cholesky | solution.py:44
  880.6 4.1 while.6
  885.4 20.5 %custom-call.32 = f32[2,128,128]{1,2,0:T(8,128)S(1)} custom-call(f32[2,128,128]{2,1,0:T(8,128)} %copy-done.16), custom_call_target="InvertDiagBlocksLowerTriangular" | custom-call | tf_op jit(solution)/shard_map/jit(_cho_solve)/triangular_solve | solution.py:44
  (150 shorter events, 74.1 us)
Async XLA Ops:
  7.2 303.6 %copy-start = (f32[512,1024]{1,0:T(8,128)S(1)}, f32[512,1024]{1,0:T(8,128)}, u32[]{:S(2)}) copy-start(f32[512,1024]{1,0:T(8,128)} %param.9) | copy-start | bytes 6291460
  7.2 87.9 %all-reduce.9.cloned.1.call-start = ((), (), s32[]{:S(2)}) async-start(), calls=%async_computation | async-start | bytes 2097152 | tf_op jit(solution)/shard_map/psum | solution.py:29
  17.9 81.3 %copy-start.12 = (f32[256,1024]{1,0:T(8,128)S(1)}, f32[256,1024]{1,0:T(8,128)}, u32[]{:S(2)}) copy-start(f32[256,1024]{1,0:T(8,128)} %param.8) | copy-start | bytes 3145732
  17.9 223.7 %all-reduce.11.cloned.1.call-start = ((), (), s32[]{:S(2)}) async-start(), calls=%async_computation.1 | async-start | bytes 524288 | tf_op jit(solution)/shard_map/psum | solution.py:31
  99.2 362.1 %all-reduce.19.cloned.1.call-start = ((), (), s32[]{:S(2)}) async-start(), calls=%async_computation.5 | async-start | bytes 5242880 | tf_op jit(solution)/shard_map/psum | solution.py:30
  109.9 198.5 %copy-start.4 = (f32[1024,256]{1,0:T(8,128)S(1)}, f32[1024,256]{1,0:T(8,128)}, u32[]{:S(2)}) copy-start(f32[1024,256]{1,0:T(8,128)} %all-reduce.9.cloned.1.call-done) | copy-start | bytes 3145732
  243.7 0.7 copy-start.13
  280.0 2.0 copy-start.10
  287.1 0.7 copy-start.17
  309.1 1.7 copy-start.5
  313.6 302.4 %all-reduce.17.cloned.1.call-start = ((), (), s32[]{:S(2)}) async-start(), calls=%async_computation.4 | async-start | bytes 2097152 | tf_op jit(solution)/shard_map/psum | solution.py:28
  313.6 16.9 %copy-start.2 = (f32[512,2048]{1,0:T(8,128)S(1)}, f32[512,2048]{1,0:T(8,128)}, u32[]{:S(2)}) copy-start(f32[512,2048]{1,0:T(8,128)} %param.10) | copy-start | bytes 12582916
  330.6 10.7 %copy-start.6 = (f32[128,1024]{1,0:T(8,128)S(1)}, f32[128,1024]{1,0:T(8,128)}, u32[]{:S(2)}) copy-start(f32[128,1024]{1,0:T(8,128)} %copy-done.5) | copy-start | bytes 1572868
  338.5 348.0 %all-reduce.13.cloned.1.call-start = ((), (), s32[]{:S(2)}) async-start(), calls=%async_computation.2 | async-start | bytes 524288 | tf_op jit(solution)/shard_map/psum | solution.py:32
  523.6 92.4 %copy-start.9 = (f32[512,256]{0,1:T(8,128)S(1)}, f32[512,256]{0,1:T(8,128)}, u32[]{:S(2)}) copy-start(f32[512,256]{0,1:T(8,128)} %get-tuple-element.72) | copy-start | bytes 1572868
  528.5 308.4 %all-reduce.15.cloned.1.call-start = ((), (), s32[]{:S(2)}) async-start(), calls=%async_computation.3 | async-start | bytes 1048576 | tf_op jit(solution)/shard_map/psum | solution.py:38
  688.5 11.7 %copy-start.14 = (f32[256,256]{1,0:T(8,128)}, f32[256,256]{1,0:T(8,128)S(1)}, u32[]{:S(2)}) copy-start(f32[256,256]{1,0:T(8,128)S(1)} %fusion.14) | copy-start | bytes 786436
  750.6 2.4 copy-start.1
  755.1 2.9 copy-start.3
  755.3 1.3 copy-start.7
  838.7 67.1 %copy-start.8 = (f32[512,256]{0,1:T(8,128)S(1)}, f32[512,256]{0,1:T(8,128)}, u32[]{:S(2)}) copy-start(f32[512,256]{0,1:T(8,128)} %all-reduce.15.cloned.1.call-done) | copy-start | bytes 1572868
  840.6 0.7 copy-start.15
  877.7 1.9 copy-start.11
  884.7 0.7 copy-start.16
Sparse Core Ops, SparseCore 0:
  18.1 76.9 all-reduce.8
  99.3 142.3 all-reduce.10
  313.7 147.4 all-reduce.18
  465.9 150.0 all-reduce.16
  618.9 67.5 all-reduce.12
  762.7 74.2 all-reduce.14
where the time goes:
time: 929 us; the launch traced here: 916 us
  waiting for transfers between devices  552 us (59%)
  other arithmetic  225 us (24%)
  matrix products  86.6 us (9%)
  local copies, waits for them, and re-layouts  28.3 us (3%)
  between operations  20.2 us (2%)
    psum x1, waiting for transfers between devices, per_device(): gram_y = lax.psum(inner_rows(range_full, range_full) / rows_total, 'cell')  132 us
    psum x1, waiting for transfers between devices, per_device(): co_full = lax.psum(co_term, 'cell')  116 us
    psum x1, waiting for transfers between devices, per_device(): sketch_z = lax.psum(core_term, ('cell', 'tm'))  87.1 us
    psum x1, waiting for transfers between devices, per_device(): range_full = lax.psum(range_term, 'tm')  77.1 us
    psum x1, waiting for transfers between devices, per_device(): right_image = lax.psum(inner_cols(core_right, co_basis), 'tm')  73.2 us
    psum x1, waiting for transfers between devices, per_device(): gram_w = lax.psum(inner_cols(co_full, co_full) / cols_total, 'tm')  66.9 us
    dot_general x5, matrix products, product(): jnp.dot(left, right, precision=lax.Precision.HIGHEST, preferred_element_t...  41.7 us
    another operation x7, other arithmetic, per_device(): jnp.linalg.cholesky(gram_right)  34.8 us
  transfers between devices with their start and end apart: 6, of which 6 were waited for; matrix products, arithmetic and copies ran while one was open for 12% of the time, Pallas kernels for 0%

commit v1 on v0

v1 whole, which is shorter than its diff:
```python
import functools
import math

import jax
import jax.numpy as jnp
from jax import lax
from jax.experimental import pallas as pl
from jax.experimental.pallas import tpu as pltpu
from jax.sharding import PartitionSpec as P

MESH = pl.DeviceIdType.MESH
F32 = jnp.float32
BF16 = jnp.bfloat16
NN = (((1,), (0,)), ((), ()))
NT = (((1,), (1,)), ((), ()))
TN = (((0,), (0,)), ((), ()))


def split(value):
    high = value.astype(BF16)
    low = (value - high.astype(F32)).astype(BF16)
    return high, low


def mm(left, right, dims):
    return lax.dot_general(left, right, dims, preferred_element_type=F32)


def mm3(left, right, dims):
    return mm(left[0], right[0], dims) + (mm(left[0], right[1], dims) + mm(left[1], right[0], dims))


def mm3f(left, right, dims):
    return mm3(split(left), split(right), dims)


def mmh(left, right, dims):
    return lax.dot_general(left, right, dims, precision=lax.Precision.HIGHEST, preferred_element_type=F32)


class Reduce:
    def __init__(self, net, source, out, core_in, total, relay_a, relay_b, in_l, in_r, y_in, z_in, rows):
        self.net, self.source, self.out = net, source, out
        self.core_in, self.total = core_in, total
        self.ra, self.rb, self.in_l, self.in_r = relay_a, relay_b, in_l, in_r
        self.y_in, self.z_in, self.r = y_in, z_in, rows

    def core_send(self):
        n, r = self.net, self.r
        self.c = n.copy(self.source.at[n.rows((1 - n.c) * 16 * r, 16 * r)], self.core_in, n.partner)

    def core_done(self):
        n, r = self.net, self.r
        self.c.wait_recv()
        self.total[...] = self.source[n.rows(n.c * 16 * r, 16 * r), :] + self.core_in[...]
        self.ring = RingScatter(n, "x", self.total, 4 * r, self.ra, self.rb, self.in_l, self.in_r)
        self.ring.first()
        self.ring.second()
        self.ring.third()

    def x_mid(self):
        self.ring.mid()

    def x_done(self):
        n, r = self.net, self.r
        self.ring.finish()
        base = n.x * 4 * r
        own = n.rows(base, 4 * r)
        self.total[own, :] = self.total[own, :] + (self.in_l[...] + self.in_r[...])
        self.y = []
        for k in (1, 2, 3):
            q = lax.rem(n.y + k, 4)
            self.y.append(n.copy(self.total.at[n.rows(base + q * r, r)], self.y_in.at[k - 1], n.at(y=q)))

    def y_done(self):
        n, r = self.net, self.r
        for c in self.y:
            c.wait_recv()
        own = n.rows(n.x * 4 * r + n.y * r, r)
        self.z_in[n.z] = (self.total[own, :] + self.y_in[0]) + (self.y_in[1] + self.y_in[2])
        self.zc = []
        for k in (1, 2, 3):
            self.zc.append(n.copy(self.z_in.at[n.z], self.z_in.at[n.z], n.at(z=lax.rem(n.z + k, 4))))

    def z_done(self):
        n, r = self.net, self.r
        for c in self.zc:
            c.wait_recv()
        offset = n.c * 16 * r + n.x * 4 * r + n.y * r
        own = n.rows(offset, r)
        self.out[own, :] = (self.z_in[0] + self.z_in[1]) + (self.z_in[2] + self.z_in[3])
        self.yc = []
        for k in (1, 2, 3):
            self.yc.append(n.copy(self.out.at[own], self.out.at[own], n.at(y=lax.rem(n.y + k, 4))))

    def y_gathered(self):
        n, r = self.net, self.r
        for c in self.yc:
            c.wait_recv()
        self.gather = RingGather(n, "x", self.out, n.c * 16 * r, 4 * r)
        self.gather.first()

    def x_gather_mid(self):
        self.gather.mid()

    def x_gathered(self):
        n, r = self.net, self.r
        self.gather.finish()
        own = n.rows(n.c * 16 * r, 16 * r)
        self.c2 = n.copy(self.out.at[own], self.out.at[own], n.partner)

    def core_gathered(self):
        self.c2.wait_recv()


class RingScatter:
    def __init__(self, net, axis, parts, size, relay_a, relay_b, in_l, in_r):
        self.n, self.parts, self.size, self.half = net, parts, size, size // 2
        me = getattr(net, axis)
        self.far, self.right, self.left = lax.rem(me + 2, 4), lax.rem(me + 1, 4), lax.rem(me + 3, 4)
        self.to_right, self.to_left = net.at(**{axis: self.right}), net.at(**{axis: self.left})
        self.ra, self.rb, self.in_l, self.in_r = relay_a, relay_b, in_l, in_r

    def piece(self, q, side):
        return self.n.rows(q * self.size + side * self.half, self.half)

    def first(self):
        self.c0 = self.n.copy(self.parts.at[self.piece(self.far, 0)], self.ra, self.to_right)
        self.c1 = self.n.copy(self.parts.at[self.piece(self.far, 1)], self.rb, self.to_left)

    def second(self):
        h = self.half
        self.c2 = self.n.copy(self.parts.at[self.piece(self.right, 1)], self.in_l.at[pl.ds(h, h)], self.to_right)

    def third(self):
        h = self.half
        self.c3 = self.n.copy(self.parts.at[self.piece(self.left, 0)], self.in_r.at[pl.ds(0, h)], self.to_left)

    def mid(self):
        h = self.half
        self.c0.wait_recv()
        at = self.piece(self.right, 0)
        self.parts[at, :] = self.parts[at, :] + self.ra[...]
        self.c4 = self.n.copy(self.parts.at[at], self.in_l.at[pl.ds(0, h)], self.to_right)
        self.c1.wait_recv()
        at = self.piece(self.left, 1)
        self.parts[at, :] = self.parts[at, :] + self.rb[...]
        self.c5 = self.n.copy(self.parts.at[at], self.in_r.at[pl.ds(h, h)], self.to_left)

    def finish(self):
        for c in (self.c2, self.c3, self.c4, self.c5):
            c.wait_recv()


class RingGather:
    def __init__(self, net, axis, out, base, size):
        self.n, self.out, self.base, self.size, self.half = net, out, base, size, size // 2
        self.me = getattr(net, axis)
        self.right, self.left = lax.rem(self.me + 1, 4), lax.rem(self.me + 3, 4)
        self.to_right, self.to_left = net.at(**{axis: self.right}), net.at(**{axis: self.left})

    def first(self):
        own = self.n.rows(self.base + self.me * self.size, self.size)
        self.g0 = self.n.copy(self.out.at[own], self.out.at[own], self.to_right)
        self.g1 = self.n.copy(self.out.at[own], self.out.at[own], self.to_left)

    def mid(self):
        self.g0.wait_recv()
        at = self.n.rows(self.base + self.left * self.size, self.half)
        self.g2 = self.n.copy(self.out.at[at], self.out.at[at], self.to_right)
        self.g1.wait_recv()
        at = self.n.rows(self.base + self.right * self.size + self.half, self.half)
        self.g3 = self.n.copy(self.out.at[at], self.out.at[at], self.to_left)

    def finish(self):
        self.g2.wait_recv()
        self.g3.wait_recv()


class Net:
    def __init__(self, send_sem, recv_sem):
        cell, tm = lax.axis_index("cell"), lax.axis_index("tm")
        self.x, self.zh, self.c = cell // 4, lax.rem(cell // 2, 2), lax.rem(cell, 2)
        self.y, self.zl = tm // 2, lax.rem(tm, 2)
        self.z = self.zh * 2 + self.zl
        self.partner = self.at(c=1 - self.c)
        self.send_sem, self.recv_sem = send_sem, recv_sem
        self.copies = []

    def at(self, x=None, y=None, z=None, c=None):
        x = self.x if x is None else x
        y = self.y if y is None else y
        c = self.c if c is None else c
        zh, zl = (self.zh, self.zl) if z is None else (z // 2, lax.rem(z, 2))
        return ((x * 2 + zh) * 2 + c, y * 2 + zl)

    def rows(self, start, size):
        return pl.ds(pl.multiple_of(start, 8), size)

    def copy(self, src, dst, device):
        k = len(self.copies)
        c = pltpu.make_async_remote_copy(
            src_ref=src, dst_ref=dst, send_sem=self.send_sem.at[k], recv_sem=self.recv_sem.at[k],
            device_id=device, device_id_type=MESH,
        )
        c.start()
        self.copies.append(c)
        return c


COPIES = 80


def order(k):
    return lax.rem(2 + 3 * k + (k // 2) * (3 + 2 * lax.rem(k, 2)), 4)


def exchange_kernel(
    window, range_test, co_test, core_left, core_right,
    y_out, w_out, cycw_out, late_out,
    w_stage, w_hi, w_lo, rt_f, ct_f, cl_f, cr_f, rt_hi, rt_lo, ct_hi, ct_lo, cl_hi, cl_lo, cr_hi, cr_lo,
    co, co_hi, co_lo, co_core, co_ra, co_rb, co_l, co_r, co_z,
    rg, rg_hi, rg_lo, rg_ra, rg_rb, rg_l, rg_r, rg_z,
    v_hi, v_lo, z_hi, z_lo,
    ar1, a1_core, a1_tot, a1_ra, a1_rb, a1_l, a1_r, a1_y, a1_z,
    ar2, a2_core, a2_tot, a2_ra, a2_rb, a2_l, a2_r, a2_y, a2_z,
    in_sem, send_sem, recv_sem,
):
    n = Net(send_sem, recv_sem)
    barrier = pltpu.get_barrier_semaphore()
    peers = [n.partner]
    for k in (1, 2, 3):
        peers += [n.at(x=lax.rem(n.x + k, 4)), n.at(y=lax.rem(n.y + k, 4)), n.at(z=lax.rem(n.z + k, 4))]
    for peer in peers:
        pl.semaphore_signal(barrier, inc=1, device_id=peer, device_id_type=MESH)

    def column_block(s):
        return ((1 - s // 4) * (1 - n.c) + (s // 4) * n.c) * 4 + lax.rem(n.x + order(lax.rem(s, 4)), 4)

    def w_copy(s):
        return pltpu.make_async_copy(
            window.at[:, pl.ds(pl.multiple_of(column_block(s) * 256, 256), 256)], w_stage.at[s], in_sem.at[s])

    loads = [pltpu.make_async_copy(a, b, in_sem.at[8 + i]) for i, (a, b) in enumerate(
        ((co_test, ct_f), (range_test, rt_f), (core_left, cl_f), (core_right, cr_f)))]
    loads[0].start()
    for s in range(8):
        w_copy(s).start()
    for c in loads[1:]:
        c.start()

    loads[0].wait()
    ct_hi[...], ct_lo[...] = split(ct_f[...])

    def co_block(s):
        w_copy(s).wait()
        block = column_block(s)
        cols = pl.ds(pl.multiple_of(block * 256, 256), 256)
        for part in range(2):
            rows = pl.ds(part * 512, 512)
            high, low = split(w_stage[s, rows, :])
            w_hi[rows, cols] = high
            w_lo[rows, cols] = low
        value = mm3((ct_hi[...], ct_lo[...]), (w_hi[:, cols], w_lo[:, cols]), NN)
        co_hi[block], co_lo[block] = split(value)
        at = n.rows(block * 512, 256)
        co[at, :] = value[:, :128]
        at = n.rows(block * 512 + 256, 256)
        co[at, :] = value[:, 128:]

    co_copies = []
    pl.loop(0, 4)(co_block)
    pl.semaphore_wait(barrier, 10)
    co_core_copy = n.copy(co.at[n.rows((1 - n.c) * 2048, 2048)], co_core, n.partner)
    pl.loop(4, 8)(co_block)

    loads[1].wait()
    rt_hi[...], rt_lo[...] = split(rt_f[...])
    co_core_copy.wait_recv()
    co_core[...] = co_core[...] + co[n.rows(n.c * 2048, 2048), :]
    co_ring = RingScatter(n, "x", co_core, 512, co_ra, co_rb, co_l, co_r)
    co_ring.first()
    co_ring.second()
    co_ring.third()

    rg_ring = RingScatter(n, "y", rg, 256, rg_ra, rg_rb, rg_l, rg_r)

    def range_block(k):
        rows = n.rows(lax.rem(n.y + order(k), 4) * 256, 256)
        value = mm3((w_hi[rows, :], w_lo[rows, :]), (rt_hi[...], rt_lo[...]), NN)
        rg[rows, :] = value
        rg_hi[rows, :], rg_lo[rows, :] = split(value)

    pl.loop(0, 3)(range_block)
    rg_ring.first()
    rg_ring.second()
    rg_ring.third()
    pl.loop(3, 4)(range_block)
    co_ring.mid()

    loads[2].wait()
    cl_hi[...], cl_lo[...] = split(cl_f[...])
    ar1[pl.ds(0, 512), :] = mm3((cl_hi[...], cl_lo[...]), (rg_hi[...], rg_lo[...]), NN)
    loads[3].wait()
    cr_hi[...], cr_lo[...] = split(cr_f[...])
    rg_ring.mid()
    ar1[pl.ds(512, 512), :] = jnp.zeros((512, 256), F32)

    def cw_block(k):
        cols = pl.ds(pl.multiple_of(k * 256, 256), 256)
        ar1[pl.ds(512, 512), :] += mm3((cr_hi[:, cols], cr_lo[:, cols]), (co_hi[k], co_lo[k]), NT)

    pl.loop(0, 8)(cw_block)
    first = Reduce(n, ar1, cycw_out, a1_core, a1_tot, a1_ra, a1_rb, a1_l, a1_r, a1_y, a1_z, 32)
    first.core_send()

    def v_block(k):
        rows = n.rows(k * 256, 256)
        value = mm3((w_hi[rows, :], w_lo[rows, :]), (cr_hi[...], cr_lo[...]), NT)
        v_hi[rows, :], v_lo[rows, :] = split(value)

    pl.loop(0, 1)(v_block)
    co_ring.finish()
    own = n.rows(n.x * 512, 512)
    co_core[own, :] = co_core[own, :] + (co_l[...] + co_r[...])
    co_z_copy = n.copy(co_core.at[n.rows(n.x * 512 + (1 - n.zh) * 256, 256)], co_z, n.at(z=lax.rem(n.z + 2, 4)))
    first.core_done()
    pl.loop(1, 2)(v_block)
    rg_ring.finish()
    own = n.rows(n.y * 256, 256)
    rg[own, :] = rg[own, :] + (rg_l[...] + rg_r[...])
    rg_z_copy = n.copy(rg.at[n.rows(n.y * 256 + (1 - n.zl) * 128, 128)], rg_z, n.at(z=n.zh * 2 + 1 - n.zl))
    co_z_copy.wait_recv()
    w_block = n.c * 8 + n.x * 2 + n.zh
    w_own = n.rows(w_block * 256, 256)
    w_out[w_own, :] = co_core[n.rows(n.x * 512 + n.zh * 256, 256), :] + co_z[...]
    w_z_copy = n.copy(w_out.at[w_own], w_out.at[w_own], n.at(z=lax.rem(n.z + 2, 4)))
    first.x_mid()
    pl.loop(2, 3)(v_block)
    rg_z_copy.wait_recv()
    y_own = n.rows(n.y * 256 + n.zl * 128, 128)
    y_out[y_own, :] = rg[y_own, :] + rg_z[...]
    y_z_copy = n.copy(y_out.at[y_own], y_out.at[y_own], n.at(z=n.zh * 2 + 1 - n.zl))
    first.x_done()

    part = split(y_out[y_own, :])
    ar2[pl.ds(0, 256), :] = mm3(part, part, TN) * (1.0 / 16384)
    part = split(w_out[w_own, :])
    ar2[pl.ds(256, 256), :] = mm3(part, part, NT) * (1.0 / 16384)
    w_z_copy.wait_recv()
    w_gather = RingGather(n, "x", w_out, n.c * 2048, 512)
    w_gather.first()
    pl.loop(3, 4)(v_block)
    first.y_done()
    y_z_copy.wait_recv()
    y_gather = RingGather(n, "y", y_out, 0, 256)
    y_gather.first()

    def z_block(k):
        rows = n.rows(k * 256, 256)
        value = mm3((cl_hi[rows, :], cl_lo[rows, :]), (v_hi[...], v_lo[...]), NN)
        z_hi[rows, :], z_lo[rows, :] = split(value)

    pl.loop(0, 2)(z_block)
    first.z_done()
    w_gather.mid()
    first.y_gathered()
    y_gather.mid()
    first.x_gather_mid()
    first.x_gathered()
    w_gather.finish()
    w_half = n.rows(n.c * 2048, 2048)
    w_core_copy = n.copy(w_out.at[w_half], w_out.at[w_half], n.partner)
    first.core_gathered()

    middle = mm3((z_hi[...], z_lo[...]), split(cycw_out[pl.ds(512, 512), :]), NN)
    ar2[pl.ds(512, 256), :] = mm3f(cycw_out[pl.ds(0, 512), :], middle, TN)
    second = Reduce(n, ar2, late_out, a2_core, a2_tot, a2_ra, a2_rb, a2_l, a2_r, a2_y, a2_z, 24)
    second.core_send()
    second.core_done()
    second.x_mid()
    second.x_done()
    second.y_done()
    second.z_done()
    second.y_gathered()
    second.x_gather_mid()
    second.x_gathered()
    y_gather.finish()
    w_core_copy.wait_recv()
    second.core_gathered()
    for c in n.copies:
        c.wait_send()


def exchange(window, range_test, co_test, core_left, core_right):
    def f(*shape):
        return pltpu.VMEM(shape, F32)

    def b(*shape):
        return pltpu.VMEM(shape, BF16)

    def reduce_bufs(r):
        return [f(16 * r, 256), f(16 * r, 256), f(2 * r, 256), f(2 * r, 256), f(4 * r, 256), f(4 * r, 256),
                f(3, r, 256), f(4, r, 256)]

    scratch = [
        f(8, 1024, 256), b(1024, 2048), b(1024, 2048), f(2048, 256), f(256, 1024), f(512, 1024), f(512, 2048),
        b(2048, 256), b(2048, 256), b(256, 1024), b(256, 1024), b(512, 1024), b(512, 1024), b(512, 2048), b(512, 2048),
        f(4096, 128), b(8, 256, 256), b(8, 256, 256), f(2048, 128), f(256, 128), f(256, 128), f(512, 128), f(512, 128), f(256, 128),
        f(1024, 256), b(1024, 256), b(1024, 256), f(128, 256), f(128, 256), f(256, 256), f(256, 256), f(128, 256),
        b(1024, 512), b(1024, 512), b(512, 512), b(512, 512),
        f(1024, 256), *reduce_bufs(32),
        f(768, 256), *reduce_bufs(24),
        pltpu.SemaphoreType.DMA((12,)), pltpu.SemaphoreType.DMA((COPIES,)), pltpu.SemaphoreType.DMA((COPIES,)),
    ]
    return pl.pallas_call(
        exchange_kernel,
        out_shape=[jax.ShapeDtypeStruct(s, F32) for s in ((1024, 256), (4096, 128), (1024, 256), (768, 256))],
        in_specs=[pl.BlockSpec(memory_space=pl.ANY)] * 5,
        out_specs=[pl.BlockSpec(memory_space=pltpu.VMEM)] * 4,
        scratch_shapes=scratch,
        compiler_params=pltpu.CompilerParams(collective_id=0, has_side_effects=True, vmem_limit_bytes=67043328),
        name="exchange",
    )(window, range_test, co_test, core_left, core_right)


QUAD = 4


def factor_panel(tiles):
    lane = lax.broadcasted_iota(jnp.int32, (8, 128), 1)
    sub = lax.broadcasted_iota(jnp.int32, (8, 128), 0)
    group = (lane // 32) * 32
    p = list(tiles)
    e = [jnp.where(sub + 8 * t == lane - group, 1.0, 0.0).astype(F32) for t in range(4)]
    pivots = [None] * 32

    def row(x, s):
        return jnp.broadcast_to(x[s:s + 1, :], (8, 128))

    for j in range(0, 32, QUAD):
        t0 = j // 8
        cols = [[jnp.take_along_axis(p[t], group + (j + k), axis=1) for t in range(t0, 4)] for k in range(QUAD)]
        rows = [row(p[t0], j % 8 + k) for k in range(QUAD)]
        rows_e = [row(e[t0], j % 8 + k) for k in range(QUAD)]
        s = [[row(cols[k][0], j % 8 + l) for l in range(QUAD)] for k in range(QUAD)]
        coefs = []
        for k in range(QUAD):
            d = s[k][k]
            pivots[j + k] = d
            inv = 1.0 / d
            for l in range(k + 1, QUAD):
                f = s[k][l] * inv
                for m in range(l, QUAD):
                    s[l][m] = s[l][m] - s[k][m] * f
                cols[l] = [a - b * f for a, b in zip(cols[l], cols[k])]
                rows[l] = rows[l] - rows[k] * f
                rows_e[l] = rows_e[l] - rows_e[k] * f
            coefs.append(inv)
        for i, t in enumerate(range(t0, 4)):
            for k in range(QUAD):
                coef = cols[k][i] * coefs[k]
                if t == t0:
                    coef = jnp.where(sub > j % 8 + k, coef, 0.0)
                p[t] = p[t] - coef * rows[k]
                e[t] = e[t] - coef * rows_e[k]
    out = []
    for t in range(4):
        d = pivots[8 * t]
        for s in range(1, 8):
            d = jnp.where(sub == s, pivots[8 * t + s], d)
        out.append(e[t] * (1.0 / jnp.sqrt(d)))
    return out


def final_kernel(y_ref, w_ref, cycw, late, rb_ref, cb_ref, core_ref, mat):
    lane = lax.broadcasted_iota(jnp.int32, (32, 128), 1)
    eye = (lax.broadcasted_iota(jnp.int32, (256, 256), 0) == lax.broadcasted_iota(jnp.int32, (256, 256), 1)).astype(F32)
    mat[0, :, 0:256] = late[pl.ds(0, 256), :]
    mat[1, :, 0:256] = late[pl.ds(256, 256), :]
    for m in (2, 3):
        part = split(cycw[pl.ds((m - 2) * 512, 512), :])
        mat[m, :, 0:256] = mm3(part, part, TN)
    for m in range(4):
        mat[m, :, 256:512] = eye
    for p in range(8):
        r0 = 32 * p
        c0 = r0 // 128 * 128
        packed = None
        for m in range(4):
            block = mat[m, r0:r0 + 32, c0:c0 + 128]
            shift = (m * 32 - r0 % 128) % 128
            if shift:
                block = pltpu.roll(block, shift, axis=1)
            packed = block if packed is None else jnp.where(lane // 32 == m, block, packed)
        inverse = jnp.concatenate(factor_panel([packed[8 * t:8 * t + 8, :] for t in range(4)]), axis=0)
        left = jnp.concatenate([jnp.where(lane // 32 == m, inverse, 0.0) for m in range(4)], axis=0)
        right = jnp.concatenate([mat[m, r0:r0 + 32, :] for m in range(4)], axis=0)
        upper = mmh(left, right, NN)
        for m in range(4):
            mat[m, r0:r0 + 32, :] = upper[32 * m:32 * m + 32, :]
        if p == 7:
            break
        b0 = (r0 + 32) // 128 * 128
        e1 = 256 + (r0 + 32 + 127) // 128 * 128
        for m in range(4):
            u = upper[32 * m:32 * m + 32, :]
            ut = u[:, b0:256].T[r0 + 32 - b0:, :]
            mat[m, r0 + 32:, b0:e1] = mat[m, r0 + 32:, b0:e1] - mmh(ut, u[:, b0:e1], NN)
    keep = lax.broadcasted_iota(jnp.int32, (256, 256), 0) <= lax.broadcasted_iota(jnp.int32, (256, 256), 1)
    y_inv = split(mat[0, :, 256:512])
    w_inv = split(mat[1, :, 256:512])
    for k in range(4):
        rb_ref[256 * k:256 * k + 256, :] = mm3(split(y_ref[256 * k:256 * k + 256, :]), y_inv, NT)
    for k in range(16):
        cb_ref[:, 128 * k:128 * k + 128] = mm3(w_inv, split(w_ref[256 * k:256 * k + 256, :]), NN)
    up_y = jnp.where(keep, mat[0, :, 0:256], 0.0)
    up_w = jnp.where(keep, mat[1, :, 0:256], 0.0)
    l_inv = mat[2, :, 256:512]
    r_inv = mat[3, :, 256:512]
    left = mmh(up_y, mmh(l_inv, l_inv, TN), NN)
    right = mmh(mmh(r_inv, r_inv, TN), up_w, NT)
    core_ref[...] = mmh(mmh(left, late[pl.ds(512, 256), :], NN), right, NN) * 16384.0


def final(y, w, cycw, late):
    return pl.pallas_call(
        final_kernel,
        out_shape=[jax.ShapeDtypeStruct(s, F32) for s in ((1024, 256), (256, 2048), (256, 256))],
        in_specs=[pl.BlockSpec(memory_space=pltpu.VMEM)] * 4,
        out_specs=[pl.BlockSpec(memory_space=pltpu.VMEM)] * 3,
        scratch_shapes=[pltpu.VMEM((4, 256, 512), F32)],
        compiler_params=pltpu.CompilerParams(vmem_limit_bytes=60000000),
        name="final",
    )(y, w, cycw, late)


def per_device(window, range_test, co_test, core_left, core_right):
    return tuple(final(*exchange(window, range_test, co_test, core_left, core_right)))


def solution(mesh):
    return jax.shard_map(
        per_device,
        mesh=mesh,
        in_specs=(P("cell", "tm"), P("tm", None), P(None, "cell"), P(None, "cell"), P(None, "tm")),
        out_specs=(P("cell", None), P(None, "tm"), P()),
        check_vma=False,
    )
```

time: 929 us -> 118 us (0.13); the launches traced: 916 us -> 118 us
  waiting for transfers between devices: 552 us -> 0 us
  other arithmetic: 225 us -> 0 us
  Pallas kernels: 0 us -> 117 us
  matrix products: 86.6 us -> 0 us
  local copies, waits for them, and re-layouts: 28.3 us -> 0 us
  between operations: 20.2 us -> 0.64 us
    psum x6 -> x0, waiting for transfers between devices: 552 us -> none  [the longest x1 132 us: per_device(): gram_y = lax.psum(inner_rows(range_full, range_full) / rows_total, 'cell')]
    another operation x37 -> x0, other arithmetic: 221 us -> none  [the longest x7 34.8 us: per_device(): jnp.linalg.cholesky(gram_right)]
    pallas_call x0 -> x2, Pallas kernels: none -> 117 us  [the longest x1 92.6 us: exchange(): pl.pallas_call(exchange_kernel, out_shape=[jax.ShapeDtypeStruct(s, F32) f...]
    dot_general x12 -> x0, matrix products: 68.9 us -> none  [the longest x5 41.7 us: product(): jnp.dot(left, right, precision=lax.Precision.HIGHEST, preferred_element_t...]
    another operation x26 -> x0, matrix products: 17.7 us -> none  [the longest x3 4.47 us: per_device(): co_basis = jax.scipy.linalg.solve_triangular(lower_w, co_full, lower=True)]
    another operation x33 -> x0, local copies, waits for them, and re-layouts: 16.3 us -> none
  transfers between devices with their start and end apart: 6 -> 0, of which waited for: 6 -> 0; matrix products, arithmetic and copies ran while one was open for 12% -> 0% of each run, Pallas kernels for 0% -> 0%
where the time goes in v1:
time: 118 us
  Pallas kernels  117 us (99%)
    pallas_call x1, Pallas kernels, exchange(): pl.pallas_call(exchange_kernel, out_shape=[jax.ShapeDtypeStruct(s, F32) f...  92.6 us
    pallas_call x1, Pallas kernels, final(): pl.pallas_call(final_kernel, out_shape=[jax.ShapeDtypeStruct(s, F32) for...  24.3 us

profile of v1, /device:TPU:1, one launch (start us, length us, event | category | flops | bytes accessed | tf_op | source)
XLA Modules:
  0.0 117.6 jit_solution(2489375381760747375)
XLA Ops:
  0.6 92.6 %exchange.1 = (f32[1024,256]{1,0:T(8,128)}, f32[4096,128]{1,0:T(8,128)}, f32[1024,256]{1,0:T(8,128)}, f32[768,256]{1,0:T(8,128)}) custom-call(f32[1024,2048]{1,0:T(8,128)} %window.1, f32[2048,256]{1,0:T(8,128)} %range_test.1, f32[256,1024]{1,0:T(8,128)} %co_test.1, f32[512,1024]{1,0:T(8,128)} %core_left.1, f32[512,2048]{1,0:T(8,128)} %core_right.1), custom_call_target="tpu_custom_call" | custom-call | tf_op jit(solution)/shard_map/exchange/pallas_call | solution.py:416
  93.3 24.3 %final.1 = (f32[1024,256]{1,0:T(8,128)}, f32[256,2048]{1,0:T(8,128)}, f32[256,256]{1,0:T(8,128)}) custom-call(f32[1024,256]{1,0:T(8,128)} %get-tuple-element.7.y_ref, f32[4096,128]{1,0:T(8,128)} %get-tuple-element.8.w_ref, f32[1024,256]{1,0:T(8,128)} %get-tuple-element.9.cycw, f32[768,256]{1,0:T(8,128)} %get-tuple-element.10.late), custom_call_target="tpu_custom_call" | custom-call | tf_op jit(solution)/shard_map/final/pallas_call | solution.py:527

commit v2 on v0

v2 whole, which is shorter than its diff:
```python
import functools
import math

import jax
import jax.numpy as jnp
from jax import lax
from jax.experimental import pallas as pl
from jax.experimental.pallas import tpu as pltpu
from jax.sharding import PartitionSpec as P

MESH = pl.DeviceIdType.MESH
F32 = jnp.float32
BF16 = jnp.bfloat16
NN = (((1,), (0,)), ((), ()))
NT = (((1,), (1,)), ((), ()))
TN = (((0,), (0,)), ((), ()))


def split(value):
    high = value.astype(BF16)
    low = (value - high.astype(F32)).astype(BF16)
    return high, low


def mm(left, right, dims):
    return lax.dot_general(left, right, dims, preferred_element_type=F32)


def mm3(left, right, dims):
    return mm(left[0], right[0], dims) + (mm(left[0], right[1], dims) + mm(left[1], right[0], dims))


def mm3f(left, right, dims):
    return mm3(split(left), split(right), dims)


def mmh(left, right, dims):
    return lax.dot_general(left, right, dims, precision=lax.Precision.HIGHEST, preferred_element_type=F32)


class Net:
    def __init__(self, send_sem, recv_sem):
        cell, tm = lax.axis_index("cell"), lax.axis_index("tm")
        self.x, self.zh, self.c = cell // 4, lax.rem(cell // 2, 2), lax.rem(cell, 2)
        self.y, self.zl = tm // 2, lax.rem(tm, 2)
        self.z = self.zh * 2 + self.zl
        self.flip = self.zh * 2 + 1 - self.zl
        self.partner = self.at(c=1 - self.c)
        self.send_sem, self.recv_sem = send_sem, recv_sem
        self.copies = []

    def at(self, x=None, y=None, z=None, c=None):
        x = self.x if x is None else x
        y = self.y if y is None else y
        c = self.c if c is None else c
        zh, zl = (self.zh, self.zl) if z is None else (z // 2, lax.rem(z, 2))
        return ((x * 2 + zh) * 2 + c, y * 2 + zl)

    def step(self, axis, k):
        return getattr(self, axis) if k == 0 else lax.rem(getattr(self, axis) + k, 4)

    def rows(self, start, size):
        return pl.ds(pl.multiple_of(start, 8), size)

    def copy(self, src, dst, device):
        k = len(self.copies)
        c = pltpu.make_async_remote_copy(
            src_ref=src, dst_ref=dst, send_sem=self.send_sem.at[k], recv_sem=self.recv_sem.at[k],
            device_id=device, device_id_type=MESH,
        )
        c.start()
        self.copies.append(c)
        return c


PAIRS = [(i, j) for i in (2, 1, 3, 0) for j in (2, 1, 3, 0) if i or j]


class Reduce:
    def __init__(self, net, plane, third, rows, source, out, core_in, plane_in, third_in):
        self.net, self.plane, self.third, self.r = net, plane, third, rows
        self.source, self.out = source, out
        self.core_in, self.plane_in, self.third_in = core_in, plane_in, third_in

    def place(self, i, j):
        a, b = self.plane
        return self.net.c * 16 * self.r + (self.net.step(a, i) * 4 + self.net.step(b, j)) * self.r

    def peer(self, i, j):
        a, b = self.plane
        return self.net.at(**{a: self.net.step(a, i), b: self.net.step(b, j)})

    def core_send(self):
        n, half = self.net, 16 * self.r
        self.c = n.copy(self.source.at[n.rows((1 - n.c) * half, half)], self.core_in, n.partner)

    def core_done(self):
        n, r = self.net, self.r
        self.c.wait_recv()
        own = n.rows(n.c * 16 * r, 16 * r)
        self.source[own, :] = self.source[own, :] + self.core_in[...]
        self.p = [n.copy(self.source.at[n.rows(self.place(i, j), r)], self.plane_in.at[k], self.peer(i, j))
                  for k, (i, j) in enumerate(PAIRS)]

    def plane_done(self):
        n, r = self.net, self.r
        total = self.source[n.rows(self.place(0, 0), r), :]
        for k, c in enumerate(self.p):
            c.wait_recv()
            total = total + self.plane_in[k]
        me = getattr(n, self.third)
        self.third_in[me] = total
        self.t = [n.copy(self.third_in.at[me], self.third_in.at[me], n.at(**{self.third: n.step(self.third, k)}))
                  for k in (2, 1, 3)]

    def third_done(self):
        n, r = self.net, self.r
        for c in self.t:
            c.wait_recv()
        own = n.rows(self.place(0, 0), r)
        self.out[own, :] = (self.third_in[0] + self.third_in[1]) + (self.third_in[2] + self.third_in[3])
        self.g = [n.copy(self.out.at[own], self.out.at[own], self.peer(i, j)) for i, j in PAIRS]

    def gathered(self):
        n, half = self.net, 16 * self.r
        for c in self.g:
            c.wait_recv()
        own = n.rows(n.c * half, half)
        self.c2 = n.copy(self.out.at[own], self.out.at[own], n.partner)

    def core_gathered(self):
        self.c2.wait_recv()


COPIES = 140
ORDER = (2, 1, 3, 0)
PLANES = ((("x", "y"), "z"), (("x", "y"), "z"), (("x", "y"), "z"))


def meet(n):
    barrier = pltpu.get_barrier_semaphore()
    peers = [n.partner]
    for axis in "xyz":
        peers += [n.at(**{axis: n.step(axis, k)}) for k in (1, 2, 3)]
    planes = set(p for p, _ in PLANES)
    for a, b in sorted(planes):
        peers += [n.at(**{a: n.step(a, i), b: n.step(b, j)}) for i in (1, 2, 3) for j in (1, 2, 3)]
    if ("y", "z") not in planes:
        peers += [n.at(y=n.step("y", k), z=n.flip) for k in (1, 2, 3)]
    for peer in peers:
        pl.semaphore_signal(barrier, inc=1, device_id=peer, device_id_type=MESH)
    return barrier, len(peers)


def exchange_kernel(
    window, range_test, co_test, core_left, core_right,
    y_out, w_out, gram_out, cyw_out, z_out,
    w_stage, w_hi, w_lo, rt_f, ct_f, cl_f, cr_f, rt_hi, rt_lo, ct2, cl_hi, cl_lo, cr_hi, cr_lo,
    co, co_core, co_in, co_z, rg, rg_hi, rg_lo, rg_in, v_hi, v_lo,
    gram, g_core, g_plane, g_third, cyw, c_core, c_plane, c_third, zed, z_core, z_plane, z_third,
    in_sem, send_sem, recv_sem,
):
    n = Net(send_sem, recv_sem)
    barrier, greetings = meet(n)

    def column_block(s):
        half = 1 - n.c if s < 4 else n.c
        return half * 4 + n.step("x", ORDER[s % 4])

    def w_copy(s):
        return pltpu.make_async_copy(
            window.at[:, pl.ds(pl.multiple_of(column_block(s) * 256, 256), 256)], w_stage.at[s], in_sem.at[s])

    w_copies = [w_copy(s) for s in range(8)]
    loads = [pltpu.make_async_copy(a, b, in_sem.at[8 + i]) for i, (a, b) in enumerate(
        ((co_test, ct_f), (range_test, rt_f), (core_right, cr_f), (core_left, cl_f)))]
    loads[0].start()
    for c in w_copies + loads[1:]:
        c.start()

    loads[0].wait()
    ct2[0:256, :], ct2[256:512, :] = split(ct_f[...])

    def co_block(s):
        w_copies[s].wait()
        block = column_block(s)
        cols = pl.ds(pl.multiple_of(block * 256, 256), 256)
        w_hi[:, cols], w_lo[:, cols] = split(w_stage[s])
        both = mm(ct2[...], w_hi[:, cols], NN)
        value = (both[:256] + both[256:]) + mm(ct2[0:256, :], w_lo[:, cols], NN)
        co[n.rows(block * 512, 256), :] = value[:, :128]
        co[n.rows(block * 512 + 256, 256), :] = value[:, 128:]
        return n.rows(block * 512, 512)

    core_copies = []
    for s in range(4):
        at = co_block(s)
        if s == 0:
            pl.semaphore_wait(barrier, greetings)
        core_copies.append(n.copy(co.at[at], co_core.at[s], n.partner))
    x_copies = []
    for s in range(4):
        at = co_block(4 + s)
        core_copies[s].wait_recv()
        co[at, :] = co[at, :] + co_core[s]
        if ORDER[s]:
            x_copies.append(n.copy(co.at[at], co_in.at[s], n.at(x=n.step("x", ORDER[s]))))
    co_own = (n.c * 4 + n.x) * 512

    loads[1].wait()
    rt_hi[...], rt_lo[...] = split(rt_f[...])
    y_copies = []
    for s in range(4):
        q = n.step("y", ORDER[s])
        rows = n.rows(q * 256, 256)
        value = mm3((w_hi[rows, :], w_lo[rows, :]), (rt_hi[...], rt_lo[...]), NN)
        rg[rows, :] = value
        rg_hi[rows, :], rg_lo[rows, :] = split(value)
        for flipped in (1, 0):
            if ORDER[s] or flipped:
                z, zl = (n.flip, 1 - n.zl) if flipped else (n.z, n.zl)
                y_copies.append(n.copy(rg.at[n.rows(q * 256 + zl * 128, 128)], rg_in.at[len(y_copies)], n.at(y=q, z=z)))

    loads[2].wait()
    cr_hi[...], cr_lo[...] = split(cr_f[...])

    def v_block(k):
        rows = n.rows(k * 256, 256)
        value = mm3((w_hi[rows, :], w_lo[rows, :]), (cr_hi[...], cr_lo[...]), NT)
        v_hi[rows, :], v_lo[rows, :] = split(value)

    pl.loop(0, 2)(v_block)
    total = co[n.rows(co_own, 512), :]
    for k, c in enumerate(x_copies):
        c.wait_recv()
        total = total + co_in[k]
    co[n.rows(co_own, 512), :] = total
    zh_peer = n.at(z=n.step("z", 2))
    co_z_copy = n.copy(co.at[n.rows(co_own + (1 - n.zh) * 256, 256)], co_z, zh_peer)
    pl.loop(2, 4)(v_block)

    y_own = n.rows(n.y * 256 + n.zl * 128, 128)
    total = rg[y_own, :]
    for k, c in enumerate(y_copies):
        c.wait_recv()
        total = total + rg_in[k]
    y_out[y_own, :] = total
    y_z_copy = n.copy(y_out.at[y_own], y_out.at[y_own], n.at(z=n.flip))
    part = split(total)
    gram[pl.ds(0, 256), :] = mm3(part, part, TN) * (1.0 / 16384)
    w_own = n.rows(co_own + n.zh * 256, 256)
    co_z_copy.wait_recv()
    total = co[w_own, :] + co_z[...]
    w_out[w_own, :] = total
    w_z_copy = n.copy(w_out.at[w_own], w_out.at[w_own], zh_peer)
    part = split(total)
    gram[pl.ds(256, 256), :] = mm3(part, part, NT) * (1.0 / 16384)
    reduce_g = Reduce(n, *PLANES[0], 16, gram, gram_out, g_core, g_plane, g_third)
    reduce_g.core_send()

    loads[3].wait()
    cl_hi[...], cl_lo[...] = split(cl_f[...])
    left = (cl_hi[...], cl_lo[...])
    cyw[pl.ds(0, 512), :] = mm3(left, (rg_hi[...], rg_lo[...]), NN)
    reduce_g.core_done()
    for k in range(2):
        cols = pl.ds(k * 256, 256)
        cyw[pl.ds(512 + 256 * k, 256), :] = mm3(
            (ct2[0:256, :], ct2[256:512, :]), (v_hi[:, cols], v_lo[:, cols]), NN)
    reduce_c = Reduce(n, *PLANES[1], 32, cyw, cyw_out, c_core, c_plane, c_third)
    reduce_c.core_send()
    for k in range(2):
        cols = pl.ds(k * 256, 256)
        zed[pl.ds(512 * k, 512), :] = mm3(left, (v_hi[:, cols], v_lo[:, cols]), NN)
        if k == 0:
            reduce_c.core_done()
    reduce_z = Reduce(n, *PLANES[2], 32, zed, z_out, z_core, z_plane, z_third)
    reduce_z.core_send()
    reduce_g.plane_done()
    reduce_z.core_done()

    y_z_copy.wait_recv()
    y_half = n.rows(n.y * 256, 256)
    y_gather = [n.copy(y_out.at[y_half], y_out.at[y_half], n.at(y=n.step("y", k))) for k in (2, 1, 3)]
    w_z_copy.wait_recv()
    w_half = n.rows(co_own, 512)
    w_gather = [n.copy(w_out.at[w_half], w_out.at[w_half], n.at(x=n.step("x", k))) for k in (2, 1, 3)]
    reduce_c.plane_done()
    reduce_g.third_done()
    reduce_z.plane_done()
    reduce_c.third_done()
    reduce_z.third_done()
    reduce_g.gathered()
    for c in w_gather:
        c.wait_recv()
    w_half = n.rows(n.c * 2048, 2048)
    w_core_copy = n.copy(w_out.at[w_half], w_out.at[w_half], n.partner)
    reduce_c.gathered()
    for c in y_gather:
        c.wait_recv()
    reduce_z.gathered()
    reduce_g.core_gathered()
    w_core_copy.wait_recv()
    reduce_c.core_gathered()
    reduce_z.core_gathered()
    for c in n.copies:
        c.wait_send()


def exchange(window, range_test, co_test, core_left, core_right):
    def f(*shape):
        return pltpu.VMEM(shape, F32)

    def b(*shape):
        return pltpu.VMEM(shape, BF16)

    def reduce_bufs(r):
        return [f(32 * r, 256), f(16 * r, 256), f(15, r, 256), f(4, r, 256)]

    scratch = [
        f(8, 1024, 256), b(1024, 2048), b(1024, 2048), f(2048, 256), f(256, 1024), f(512, 1024), f(512, 2048),
        b(2048, 256), b(2048, 256), b(512, 1024), b(512, 1024), b(512, 1024), b(512, 2048), b(512, 2048),
        f(4096, 128), f(4, 512, 128), f(3, 512, 128), f(256, 128),
        f(1024, 256), b(1024, 256), b(1024, 256), f(7, 128, 256), b(1024, 512), b(1024, 512),
        *reduce_bufs(16), *reduce_bufs(32), *reduce_bufs(32),
        pltpu.SemaphoreType.DMA((12,)), pltpu.SemaphoreType.DMA((COPIES,)), pltpu.SemaphoreType.DMA((COPIES,)),
    ]
    return pl.pallas_call(
        exchange_kernel,
        out_shape=[jax.ShapeDtypeStruct(s, F32) for s in (
            (1024, 256), (4096, 128), (512, 256), (1024, 256), (1024, 256))],
        in_specs=[pl.BlockSpec(memory_space=pl.ANY)] * 5,
        out_specs=[pl.BlockSpec(memory_space=pltpu.VMEM)] * 5,
        scratch_shapes=scratch,
        compiler_params=pltpu.CompilerParams(collective_id=0, has_side_effects=True, vmem_limit_bytes=67043328),
        name="exchange",
    )(window, range_test, co_test, core_left, core_right)


QUAD = 4


def factor_panel(tiles):
    lane = lax.broadcasted_iota(jnp.int32, (8, 128), 1)
    sub = lax.broadcasted_iota(jnp.int32, (8, 128), 0)
    group = (lane // 32) * 32
    p = list(tiles)
    e = [jnp.where(sub + 8 * t == lane - group, 1.0, 0.0).astype(F32) for t in range(4)]
    pivots = [None] * 32

    def row(x, s):
        return jnp.broadcast_to(x[s:s + 1, :], (8, 128))

    for j in range(0, 32, QUAD):
        t0 = j // 8
        cols = [[jnp.take_along_axis(p[t], group + (j + k), axis=1) for t in range(t0, 4)] for k in range(QUAD)]
        rows = [row(p[t0], j % 8 + k) for k in range(QUAD)]
        rows_e = [row(e[t0], j % 8 + k) for k in range(QUAD)]
        s = [[row(cols[k][0], j % 8 + l) for l in range(QUAD)] for k in range(QUAD)]
        coefs = []
        for k in range(QUAD):
            d = s[k][k]
            pivots[j + k] = d
            inv = 1.0 / d
            for l in range(k + 1, QUAD):
                f = s[k][l] * inv
                for m in range(l, QUAD):
                    s[l][m] = s[l][m] - s[k][m] * f
                cols[l] = [a - b * f for a, b in zip(cols[l], cols[k])]
                rows[l] = rows[l] - rows[k] * f
                rows_e[l] = rows_e[l] - rows_e[k] * f
            coefs.append(inv)
        for i, t in enumerate(range(t0, 4)):
            for k in range(QUAD):
                coef = cols[k][i] * coefs[k]
                if t == t0:
                    coef = jnp.where(sub > j % 8 + k, coef, 0.0)
                p[t] = p[t] - coef * rows[k]
                e[t] = e[t] - coef * rows_e[k]
    out = []
    for t in range(4):
        d = pivots[8 * t]
        for s in range(1, 8):
            d = jnp.where(sub == s, pivots[8 * t + s], d)
        out.append(e[t] * (1.0 / jnp.sqrt(d)))
    return out


def final_kernel(y_ref, w_ref, gram, cyw, zed, rb_ref, cb_ref, core_ref, mat):
    lane = lax.broadcasted_iota(jnp.int32, (32, 128), 1)
    eye = (lax.broadcasted_iota(jnp.int32, (256, 256), 0) == lax.broadcasted_iota(jnp.int32, (256, 256), 1)).astype(F32)
    mat[0, :, 0:256] = gram[pl.ds(0, 256), :]
    mat[1, :, 0:256] = gram[pl.ds(256, 256), :]
    cy = split(cyw[pl.ds(0, 512), :])
    mat[2, :, 0:256] = mm3(cy, cy, TN)
    cw = [split(cyw[pl.ds(512 + 256 * k, 256), :]) for k in range(2)]
    mat[3, :, 0:256] = mm3(cw[0], cw[0], NT) + mm3(cw[1], cw[1], NT)
    middle = sum(mm3(split(zed[pl.ds(512 * k, 512), :]), cw[k], NT) for k in range(2))
    inner = mm3(cy, split(middle), TN)
    for m in range(4):
        mat[m, :, 256:512] = eye
    for p in range(8):
        r0 = 32 * p
        c0 = r0 // 128 * 128
        packed = None
        for m in range(4):
            block = mat[m, r0:r0 + 32, c0:c0 + 128]
            shift = (m * 32 - r0 % 128) % 128
            if shift:
                block = pltpu.roll(block, shift, axis=1)
            packed = block if packed is None else jnp.where(lane // 32 == m, block, packed)
        inverse = jnp.concatenate(factor_panel([packed[8 * t:8 * t + 8, :] for t in range(4)]), axis=0)
        left = jnp.concatenate([jnp.where(lane // 32 == m, inverse, 0.0) for m in range(4)], axis=0)
        right = jnp.concatenate([mat[m, r0:r0 + 32, :] for m in range(4)], axis=0)
        upper = mmh(left, right, NN)
        for m in range(4):
            mat[m, r0:r0 + 32, :] = upper[32 * m:32 * m + 32, :]
        if p == 7:
            break
        b0 = (r0 + 32) // 128 * 128
        e1 = 256 + (r0 + 32 + 127) // 128 * 128
        for m in range(4):
            u = upper[32 * m:32 * m + 32, :]
            ut = u[:, b0:256].T[r0 + 32 - b0:, :]
            mat[m, r0 + 32:, b0:e1] = mat[m, r0 + 32:, b0:e1] - mmh(ut, u[:, b0:e1], NN)
    keep = lax.broadcasted_iota(jnp.int32, (256, 256), 0) <= lax.broadcasted_iota(jnp.int32, (256, 256), 1)
    y_inv = split(mat[0, :, 256:512])
    w_inv = split(mat[1, :, 256:512])
    for k in range(4):
        rb_ref[256 * k:256 * k + 256, :] = mm3(split(y_ref[256 * k:256 * k + 256, :]), y_inv, NT)
    for k in range(16):
        cb_ref[:, 128 * k:128 * k + 128] = mm3(w_inv, split(w_ref[256 * k:256 * k + 256, :]), NN)
    up_y = jnp.where(keep, mat[0, :, 0:256], 0.0)
    up_w = jnp.where(keep, mat[1, :, 0:256], 0.0)
    l_inv = mat[2, :, 256:512]
    r_inv = mat[3, :, 256:512]
    left = mmh(up_y, mmh(l_inv, l_inv, TN), NN)
    right = mmh(mmh(r_inv, r_inv, TN), up_w, NT)
    core_ref[...] = mmh(mmh(left, inner, NN), right, NN) * 16384.0


def final(*parts):
    return pl.pallas_call(
        final_kernel,
        out_shape=[jax.ShapeDtypeStruct(s, F32) for s in ((1024, 256), (256, 2048), (256, 256))],
        in_specs=[pl.BlockSpec(memory_space=pltpu.VMEM)] * 5,
        out_specs=[pl.BlockSpec(memory_space=pltpu.VMEM)] * 3,
        scratch_shapes=[pltpu.VMEM((4, 256, 512), F32)],
        compiler_params=pltpu.CompilerParams(vmem_limit_bytes=60000000),
        name="final",
    )(*parts)


def per_device(window, range_test, co_test, core_left, core_right):
    return tuple(final(*exchange(window, range_test, co_test, core_left, core_right)))


def solution(mesh):
    return jax.shard_map(
        per_device,
        mesh=mesh,
        in_specs=(P("cell", "tm"), P("tm", None), P(None, "cell"), P(None, "cell"), P(None, "tm")),
        out_specs=(P("cell", None), P(None, "tm"), P()),
        check_vma=False,
    )
```

time: 929 us -> 114 us (0.12); the launches traced: 916 us -> 114 us
  waiting for transfers between devices: 552 us -> 0 us
  other arithmetic: 225 us -> 0 us
  Pallas kernels: 0 us -> 113 us
  matrix products: 86.6 us -> 0 us
  local copies, waits for them, and re-layouts: 28.3 us -> 0 us
  between operations: 20.2 us -> 0.64 us
    psum x6 -> x0, waiting for transfers between devices: 552 us -> none  [the longest x1 132 us: per_device(): gram_y = lax.psum(inner_rows(range_full, range_full) / rows_total, 'cell')]
    another operation x37 -> x0, other arithmetic: 221 us -> none  [the longest x7 34.8 us: per_device(): jnp.linalg.cholesky(gram_right)]
    pallas_call x0 -> x2, Pallas kernels: none -> 113 us  [the longest x1 88.6 us: exchange(): pl.pallas_call(exchange_kernel, out_shape=[jax.ShapeDtypeStruct(s, F32) f...]
    dot_general x12 -> x0, matrix products: 68.9 us -> none  [the longest x5 41.7 us: product(): jnp.dot(left, right, precision=lax.Precision.HIGHEST, preferred_element_t...]
    another operation x26 -> x0, matrix products: 17.7 us -> none  [the longest x3 4.47 us: per_device(): co_basis = jax.scipy.linalg.solve_triangular(lower_w, co_full, lower=True)]
    another operation x33 -> x0, local copies, waits for them, and re-layouts: 16.3 us -> none
  transfers between devices with their start and end apart: 6 -> 0, of which waited for: 6 -> 0; matrix products, arithmetic and copies ran while one was open for 12% -> 0% of each run, Pallas kernels for 0% -> 0%
where the time goes in v2:
time: 114 us
  Pallas kernels  113 us (99%)
    pallas_call x1, Pallas kernels, exchange(): pl.pallas_call(exchange_kernel, out_shape=[jax.ShapeDtypeStruct(s, F32) f...  88.6 us
    pallas_call x1, Pallas kernels, final(): pl.pallas_call(final_kernel, out_shape=[jax.ShapeDtypeStruct(s, F32) for...  24.7 us

profile of v2, /device:TPU:1, one launch (start us, length us, event | category | flops | bytes accessed | tf_op | source)
XLA Modules:
  0.0 114.0 jit_solution(17653615426775842825)
XLA Ops:
  0.6 88.6 %exchange.1 = (f32[1024,256]{1,0:T(8,128)}, f32[4096,128]{1,0:T(8,128)}, f32[512,256]{1,0:T(8,128)}, f32[1024,256]{1,0:T(8,128)}, f32[1024,256]{1,0:T(8,128)}) custom-call(f32[1024,2048]{1,0:T(8,128)} %window.1, f32[2048,256]{1,0:T(8,128)} %range_test.1, f32[256,1024]{1,0:T(8,128)} %co_test.1, f32[512,1024]{1,0:T(8,128)} %core_left.1, f32[512,2048]{1,0:T(8,128)} %core_right.1), custom_call_target="tpu_custom_call" | custom-call | tf_op jit(solution)/shard_map/exchange/pallas_call | solution.py:328
  89.3 24.7 %final.1 = (f32[1024,256]{1,0:T(8,128)}, f32[256,2048]{1,0:T(8,128)}, f32[256,256]{1,0:T(8,128)}) custom-call(f32[1024,256]{1,0:T(8,128)} %get-tuple-element.8.y_ref, f32[4096,128]{1,0:T(8,128)} %get-tuple-element.9.w_ref, f32[512,256]{1,0:T(8,128)} %get-tuple-element.10.gram, f32[1024,256]{1,0:T(8,128)} %get-tuple-element.11.cyw, ...), custom_call_target="tpu_custom_call" | custom-call | tf_op jit(solution)/shard_map/final/pallas_call | solution.py:443

commit v3 on v2

--- a/solution.py
+++ b/solution.py
@@ -73,22 +73,22 @@
         return c
 
 
-PAIRS = [(i, j) for i in (2, 1, 3, 0) for j in (2, 1, 3, 0) if i or j]
-
-
 class Reduce:
-    def __init__(self, net, plane, third, rows, source, out, core_in, plane_in, third_in):
-        self.net, self.plane, self.third, self.r = net, plane, third, rows
+    def __init__(self, net, axes, rows, source, out, core_in, first_in, second_in, third_in):
+        self.net, self.axes, self.r = net, axes, rows
         self.source, self.out = source, out
-        self.core_in, self.plane_in, self.third_in = core_in, plane_in, third_in
-
-    def place(self, i, j):
-        a, b = self.plane
-        return self.net.c * 16 * self.r + (self.net.step(a, i) * 4 + self.net.step(b, j)) * self.r
-
-    def peer(self, i, j):
-        a, b = self.plane
-        return self.net.at(**{a: self.net.step(a, i), b: self.net.step(b, j)})
+        self.core_in, self.first_in, self.second_in, self.third_in = core_in, first_in, second_in, third_in
+
+    def place(self, i=0, j=0):
+        n, (a, b, _) = self.net, self.axes
+        return n.c * 16 * self.r + (n.step(a, i) * 4 + n.step(b, j)) * self.r
+
+    def block(self, i=0):
+        n = self.net
+        return n.rows(n.c * 16 * self.r + n.step(self.axes[0], i) * 4 * self.r, 4 * self.r)
+
+    def peer(self, axis, k):
+        return self.net.at(**{axis: self.net.step(axis, k)})
 
     def core_send(self):
         n, half = self.net, 16 * self.r
@@ -99,31 +99,45 @@
         self.c.wait_recv()
         own = n.rows(n.c * 16 * r, 16 * r)
         self.source[own, :] = self.source[own, :] + self.core_in[...]
-        self.p = [n.copy(self.source.at[n.rows(self.place(i, j), r)], self.plane_in.at[k], self.peer(i, j))
-                  for k, (i, j) in enumerate(PAIRS)]
-
-    def plane_done(self):
+        self.f = [n.copy(self.source.at[self.block(k)], self.first_in.at[i], self.peer(self.axes[0], k))
+                  for i, k in enumerate((2, 1, 3))]
+
+    def first_done(self):
         n, r = self.net, self.r
-        total = self.source[n.rows(self.place(0, 0), r), :]
-        for k, c in enumerate(self.p):
+        for c in self.f:
             c.wait_recv()
-            total = total + self.plane_in[k]
-        me = getattr(n, self.third)
-        self.third_in[me] = total
-        self.t = [n.copy(self.third_in.at[me], self.third_in.at[me], n.at(**{self.third: n.step(self.third, k)}))
-                  for k in (2, 1, 3)]
+        own = self.block()
+        self.source[own, :] = (self.source[own, :] + self.first_in[0]) + (self.first_in[1] + self.first_in[2])
+        self.s = [n.copy(self.source.at[n.rows(self.place(0, k), r)], self.second_in.at[i], self.peer(self.axes[1], k))
+                  for i, k in enumerate((2, 1, 3))]
+
+    def second_done(self):
+        n, r = self.net, self.r
+        for c in self.s:
+            c.wait_recv()
+        own = n.rows(self.place(), r)
+        me = getattr(n, self.axes[2])
+        self.third_in[me] = (self.source[own, :] + self.second_in[0]) + (self.second_in[1] + self.second_in[2])
+        self.t = [n.copy(self.third_in.at[me], self.third_in.at[me], self.peer(self.axes[2], k)) for k in (2, 1, 3)]
 
     def third_done(self):
         n, r = self.net, self.r
         for c in self.t:
             c.wait_recv()
-        own = n.rows(self.place(0, 0), r)
+        own = n.rows(self.place(), r)
         self.out[own, :] = (self.third_in[0] + self.third_in[1]) + (self.third_in[2] + self.third_in[3])
-        self.g = [n.copy(self.out.at[own], self.out.at[own], self.peer(i, j)) for i, j in PAIRS]
+        self.g = [n.copy(self.out.at[own], self.out.at[own], self.peer(self.axes[1], k)) for k in (2, 1, 3)]
+
+    def second_gathered(self):
+        n = self.net
+        for c in self.g:
+            c.wait_recv()
+        own = self.block()
+        self.h = [n.copy(self.out.at[own], self.out.at[own], self.peer(self.axes[0], k)) for k in (2, 1, 3)]
 
     def gathered(self):
         n, half = self.net, 16 * self.r
-        for c in self.g:
+        for c in self.h:
             c.wait_recv()
         own = n.rows(n.c * half, half)
         self.c2 = n.copy(self.out.at[own], self.out.at[own], n.partner)
@@ -132,9 +146,9 @@
         self.c2.wait_recv()
 
 
-COPIES = 140
+COPIES = 100
 ORDER = (2, 1, 3, 0)
-PLANES = ((("x", "y"), "z"), (("x", "y"), "z"), (("x", "y"), "z"))
+AXES = (("y", "x", "z"), ("z", "x", "y"), ("z", "y", "x"))
 
 
 def meet(n):
@@ -142,11 +156,7 @@
     peers = [n.partner]
     for axis in "xyz":
         peers += [n.at(**{axis: n.step(axis, k)}) for k in (1, 2, 3)]
-    planes = set(p for p, _ in PLANES)
-    for a, b in sorted(planes):
-        peers += [n.at(**{a: n.step(a, i), b: n.step(b, j)}) for i in (1, 2, 3) for j in (1, 2, 3)]
-    if ("y", "z") not in planes:
-        peers += [n.at(y=n.step("y", k), z=n.flip) for k in (1, 2, 3)]
+    peers += [n.at(y=n.step("y", k), z=n.flip) for k in (1, 2, 3)]
     for peer in peers:
         pl.semaphore_signal(barrier, inc=1, device_id=peer, device_id_type=MESH)
     return barrier, len(peers)
@@ -157,7 +167,7 @@
     y_out, w_out, gram_out, cyw_out, z_out,
     w_stage, w_hi, w_lo, rt_f, ct_f, cl_f, cr_f, rt_hi, rt_lo, ct2, cl_hi, cl_lo, cr_hi, cr_lo,
     co, co_core, co_in, co_z, rg, rg_hi, rg_lo, rg_in, v_hi, v_lo,
-    gram, g_core, g_plane, g_third, cyw, c_core, c_plane, c_third, zed, z_core, z_plane, z_third,
+    gram, g_core, g_first, g_second, g_third, cyw, c_core, c_first, c_second, c_third, zed, z_core, z_first, z_second, z_third,
     in_sem, send_sem, recv_sem,
 ):
     n = Net(send_sem, recv_sem)
@@ -255,7 +265,7 @@
     w_z_copy = n.copy(w_out.at[w_own], w_out.at[w_own], zh_peer)
     part = split(total)
     gram[pl.ds(256, 256), :] = mm3(part, part, NT) * (1.0 / 16384)
-    reduce_g = Reduce(n, *PLANES[0], 16, gram, gram_out, g_core, g_plane, g_third)
+    reduce_g = Reduce(n, AXES[0], 16, gram, gram_out, g_core, g_first, g_second, g_third)
     reduce_g.core_send()
 
     loads[3].wait()
@@ -267,34 +277,39 @@
         cols = pl.ds(k * 256, 256)
         cyw[pl.ds(512 + 256 * k, 256), :] = mm3(
             (ct2[0:256, :], ct2[256:512, :]), (v_hi[:, cols], v_lo[:, cols]), NN)
-    reduce_c = Reduce(n, *PLANES[1], 32, cyw, cyw_out, c_core, c_plane, c_third)
+    reduce_c = Reduce(n, AXES[1], 32, cyw, cyw_out, c_core, c_first, c_second, c_third)
     reduce_c.core_send()
     for k in range(2):
         cols = pl.ds(k * 256, 256)
         zed[pl.ds(512 * k, 512), :] = mm3(left, (v_hi[:, cols], v_lo[:, cols]), NN)
         if k == 0:
             reduce_c.core_done()
-    reduce_z = Reduce(n, *PLANES[2], 32, zed, z_out, z_core, z_plane, z_third)
+    reduce_z = Reduce(n, AXES[2], 32, zed, z_out, z_core, z_first, z_second, z_third)
     reduce_z.core_send()
-    reduce_g.plane_done()
+    reduce_g.first_done()
     reduce_z.core_done()
-
     y_z_copy.wait_recv()
     y_half = n.rows(n.y * 256, 256)
     y_gather = [n.copy(y_out.at[y_half], y_out.at[y_half], n.at(y=n.step("y", k))) for k in (2, 1, 3)]
     w_z_copy.wait_recv()
     w_half = n.rows(co_own, 512)
     w_gather = [n.copy(w_out.at[w_half], w_out.at[w_half], n.at(x=n.step("x", k))) for k in (2, 1, 3)]
-    reduce_c.plane_done()
+    reduce_g.second_done()
+    reduce_c.first_done()
     reduce_g.third_done()
-    reduce_z.plane_done()
+    reduce_z.first_done()
+    reduce_c.second_done()
+    reduce_g.second_gathered()
     reduce_c.third_done()
+    reduce_z.second_done()
+    reduce_g.gathered()
+    reduce_c.second_gathered()
     reduce_z.third_done()
-    reduce_g.gathered()
     for c in w_gather:
         c.wait_recv()
     w_half = n.rows(n.c * 2048, 2048)
     w_core_copy = n.copy(w_out.at[w_half], w_out.at[w_half], n.partner)
+    reduce_z.second_gathered()
     reduce_c.gathered()
     for c in y_gather:
         c.wait_recv()
@@ -315,7 +330,7 @@
         return pltpu.VMEM(shape, BF16)
 
     def reduce_bufs(r):
-        return [f(32 * r, 256), f(16 * r, 256), f(15, r, 256), f(4, r, 256)]
+        return [f(32 * r, 256), f(16 * r, 256), f(3, 4 * r, 256), f(3, r, 256), f(4, r, 256)]
 
     scratch = [
         f(8, 1024, 256), b(1024, 2048), b(1024, 2048), f(2048, 256), f(256, 1024), f(512, 1024), f(512, 2048),
@@ -337,7 +352,7 @@
     )(window, range_test, co_test, core_left, core_right)
 
 
-QUAD = 4
+QUAD = 8
 
 
 def factor_panel(tiles):
@@ -386,7 +401,17 @@
     return out
 
 
-def final_kernel(y_ref, w_ref, gram, cyw, zed, rb_ref, cb_ref, core_ref, mat):
+def stacked(left, right):
+    both = mm(jnp.concatenate(left, axis=1), jnp.concatenate([right[0], right[0]], axis=0), NN)
+    return both + mm(left[0], right[1], NN)
+
+
+def final_kernel(
+    y_hbm, w_hbm, gram, cyw, zed, rb_hbm, cb_hbm, core_ref, mat, y_ref, w_ref, rb_ref, cb_ref, mid, in_sem, out_sem
+):
+    loads = [pltpu.make_async_copy(y_hbm, y_ref, in_sem.at[0]), pltpu.make_async_copy(w_hbm, w_ref, in_sem.at[1])]
+    for c in loads:
+        c.start()
     lane = lax.broadcasted_iota(jnp.int32, (32, 128), 1)
     eye = (lax.broadcasted_iota(jnp.int32, (256, 256), 0) == lax.broadcasted_iota(jnp.int32, (256, 256), 1)).astype(F32)
     mat[0, :, 0:256] = gram[pl.ds(0, 256), :]
@@ -395,13 +420,15 @@
     mat[2, :, 0:256] = mm3(cy, cy, TN)
     cw = [split(cyw[pl.ds(512 + 256 * k, 256), :]) for k in range(2)]
     mat[3, :, 0:256] = mm3(cw[0], cw[0], NT) + mm3(cw[1], cw[1], NT)
-    middle = sum(mm3(split(zed[pl.ds(512 * k, 512), :]), cw[k], NT) for k in range(2))
-    inner = mm3(cy, split(middle), TN)
     for m in range(4):
         mat[m, :, 256:512] = eye
     for p in range(8):
         r0 = 32 * p
         c0 = r0 // 128 * 128
+        e1 = 256 + (r0 + 32 + 127) // 128 * 128
+        rows = slice(64 * p, 64 * p + 64)
+        mid[rows, :] = (mm3(split(zed[64 * p:64 * p + 64, :]), cw[0], NT)
+                        + mm3(split(zed[512 + 64 * p:512 + 64 * p + 64, :]), cw[1], NT))
         packed = None
         for m in range(4):
             block = mat[m, r0:r0 + 32, c0:c0 + 128]
@@ -411,42 +438,60 @@
             packed = block if packed is None else jnp.where(lane // 32 == m, block, packed)
         inverse = jnp.concatenate(factor_panel([packed[8 * t:8 * t + 8, :] for t in range(4)]), axis=0)
         left = jnp.concatenate([jnp.where(lane // 32 == m, inverse, 0.0) for m in range(4)], axis=0)
-        right = jnp.concatenate([mat[m, r0:r0 + 32, :] for m in range(4)], axis=0)
-        upper = mmh(left, right, NN)
+        right = jnp.concatenate([mat[m, r0:r0 + 32, c0:e1] for m in range(4)], axis=0)
+        upper = stacked(split(left), split(right))
         for m in range(4):
-            mat[m, r0:r0 + 32, :] = upper[32 * m:32 * m + 32, :]
+            mat[m, r0:r0 + 32, c0:e1] = upper[32 * m:32 * m + 32, :]
         if p == 7:
             break
         b0 = (r0 + 32) // 128 * 128
-        e1 = 256 + (r0 + 32 + 127) // 128 * 128
+        u_high, u_low = split(upper[:, b0 - c0:])
+        below = split(upper[:, b0 - c0:256 - c0].T[r0 + 32 - b0:, :])
+        zero = jnp.zeros((32, e1 - b0), BF16)
         for m in range(4):
-            u = upper[32 * m:32 * m + 32, :]
-            ut = u[:, b0:256].T[r0 + 32 - b0:, :]
-            mat[m, r0 + 32:, b0:e1] = mat[m, r0 + 32:, b0:e1] - mmh(ut, u[:, b0:e1], NN)
+            mine = [jnp.concatenate([u[32 * m:32 * m + 32] if k == m else zero for k in range(4)], axis=0)
+                    for u in (u_high, u_low)]
+            mat[m, r0 + 32:, b0:e1] = mat[m, r0 + 32:, b0:e1] - stacked(below, mine)
     keep = lax.broadcasted_iota(jnp.int32, (256, 256), 0) <= lax.broadcasted_iota(jnp.int32, (256, 256), 1)
     y_inv = split(mat[0, :, 256:512])
     w_inv = split(mat[1, :, 256:512])
-    for k in range(4):
-        rb_ref[256 * k:256 * k + 256, :] = mm3(split(y_ref[256 * k:256 * k + 256, :]), y_inv, NT)
-    for k in range(16):
-        cb_ref[:, 128 * k:128 * k + 128] = mm3(w_inv, split(w_ref[256 * k:256 * k + 256, :]), NN)
+    for c in loads:
+        c.wait()
+    stores = []
+    for k in range(2):
+        rows = slice(512 * k, 512 * k + 512)
+        rb_ref[rows, :] = mm3(split(y_ref[rows, :]), y_inv, NT)
+        stores.append(pltpu.make_async_copy(rb_ref.at[rows], rb_hbm.at[rows], out_sem.at[k]))
+        stores[-1].start()
+    for k in range(8):
+        cols = slice(256 * k, 256 * k + 256)
+        block = jnp.concatenate([w_ref[512 * k:512 * k + 256, :], w_ref[512 * k + 256:512 * k + 512, :]], axis=1)
+        cb_ref[:, cols] = mm3(w_inv, split(block), NN)
+        stores.append(pltpu.make_async_copy(cb_ref.at[:, cols], cb_hbm.at[:, cols], out_sem.at[2 + k]))
+        stores[-1].start()
     up_y = jnp.where(keep, mat[0, :, 0:256], 0.0)
     up_w = jnp.where(keep, mat[1, :, 0:256], 0.0)
-    l_inv = mat[2, :, 256:512]
-    r_inv = mat[3, :, 256:512]
-    left = mmh(up_y, mmh(l_inv, l_inv, TN), NN)
-    right = mmh(mmh(r_inv, r_inv, TN), up_w, NT)
-    core_ref[...] = mmh(mmh(left, inner, NN), right, NN) * 16384.0
+    l_inv = split(mat[2, :, 256:512])
+    r_inv = split(mat[3, :, 256:512])
+    inner = mm3(cy, split(mid[...]), TN)
+    left = mm3f(up_y, mm3(l_inv, l_inv, TN), NN)
+    right = mm3f(mm3(r_inv, r_inv, TN), up_w, NT)
+    core_ref[...] = mm3f(mm3f(left, inner, NN), right, NN) * 16384.0
+    for c in stores:
+        c.wait()
 
 
 def final(*parts):
+    spec, hbm = pl.BlockSpec(memory_space=pltpu.VMEM), pl.BlockSpec(memory_space=pl.ANY)
     return pl.pallas_call(
         final_kernel,
         out_shape=[jax.ShapeDtypeStruct(s, F32) for s in ((1024, 256), (256, 2048), (256, 256))],
-        in_specs=[pl.BlockSpec(memory_space=pltpu.VMEM)] * 5,
-        out_specs=[pl.BlockSpec(memory_space=pltpu.VMEM)] * 3,
-        scratch_shapes=[pltpu.VMEM((4, 256, 512), F32)],
-        compiler_params=pltpu.CompilerParams(vmem_limit_bytes=60000000),
+        in_specs=[hbm, hbm, spec, spec, spec],
+        out_specs=[hbm, hbm, spec],
+        scratch_shapes=[pltpu.VMEM(s, F32) for s in (
+            (4, 256, 512), (1024, 256), (4096, 128), (1024, 256), (256, 2048), (512, 256))]
+        + [pltpu.SemaphoreType.DMA((2,)), pltpu.SemaphoreType.DMA((10,))],
+        compiler_params=pltpu.CompilerParams(vmem_limit_bytes=67043328),
         name="final",
     )(*parts)
 

time: 114 us -> 105 us (0.921)
  Pallas kernels: 113 us -> 104 us
    pallas_call x1, Pallas kernels: 24.7 us -> 17.8 us  [final(): pl.pallas_call(final_kernel, out_shape=[jax.ShapeDtypeStruct(s, F32) for...]
    pallas_call x1, Pallas kernels: 88.6 us -> 86.4 us  [exchange(): pl.pallas_call(exchange_kernel, out_shape=[jax.ShapeDtypeStruct(s, F32) f...]
where the time goes in v3:
time: 105 us
  Pallas kernels  104 us (99%)
    pallas_call x1, Pallas kernels, exchange(): pl.pallas_call(exchange_kernel, out_shape=[jax.ShapeDtypeStruct(s, F32) f...  86.4 us
    pallas_call x1, Pallas kernels, final(): pl.pallas_call(final_kernel, out_shape=[jax.ShapeDtypeStruct(s, F32) for...  17.8 us

profile of v3, /device:TPU:1, one launch (start us, length us, event | category | flops | bytes accessed | tf_op | source)
XLA Modules:
  0.0 105.0 jit_solution(2874198832680770482)
XLA Ops:
  0.6 86.4 %exchange.1 = (f32[1024,256]{1,0:T(8,128)}, f32[4096,128]{1,0:T(8,128)}, f32[512,256]{1,0:T(8,128)}, f32[1024,256]{1,0:T(8,128)}, f32[1024,256]{1,0:T(8,128)}) custom-call(f32[1024,2048]{1,0:T(8,128)} %window.1, f32[2048,256]{1,0:T(8,128)} %range_test.1, f32[256,1024]{1,0:T(8,128)} %co_test.1, f32[512,1024]{1,0:T(8,128)} %core_left.1, f32[512,2048]{1,0:T(8,128)} %core_right.1), custom_call_target="tpu_custom_call" | custom-call | tf_op jit(solution)/shard_map/exchange/pallas_call | solution.py:343
  87.0 17.8 %final.1 = (f32[1024,256]{1,0:T(8,128)}, f32[256,2048]{1,0:T(8,128)}, f32[256,256]{1,0:T(8,128)}) custom-call(f32[1024,256]{1,0:T(8,128)} %get-tuple-element.8.y_hbm, f32[4096,128]{1,0:T(8,128)} %get-tuple-element.9.w_hbm, f32[512,256]{1,0:T(8,128)} %get-tuple-element.10.gram, f32[1024,256]{1,0:T(8,128)} %get-tuple-element.11.cyw, ...), custom_call_target="tpu_custom_call" | custom-call | tf_op jit(solution)/shard_map/final/pallas_call | solution.py:486

commit v4 on v3

--- a/solution.py
+++ b/solution.py
@@ -148,7 +148,7 @@
 
 COPIES = 100
 ORDER = (2, 1, 3, 0)
-AXES = (("y", "x", "z"), ("z", "x", "y"), ("z", "y", "x"))
+AXES = (("y", "x", "z"), ("x", "y", "z"), ("z", "y", "x"))
 
 
 def meet(n):
@@ -156,7 +156,7 @@
     peers = [n.partner]
     for axis in "xyz":
         peers += [n.at(**{axis: n.step(axis, k)}) for k in (1, 2, 3)]
-    peers += [n.at(y=n.step("y", k), z=n.flip) for k in (1, 2, 3)]
+    peers += [n.at(x=n.step("x", k), z=n.step("z", 2)) for k in (1, 2, 3)]
     for peer in peers:
         pl.semaphore_signal(barrier, inc=1, device_id=peer, device_id_type=MESH)
     return barrier, len(peers)
@@ -166,36 +166,52 @@
     window, range_test, co_test, core_left, core_right,
     y_out, w_out, gram_out, cyw_out, z_out,
     w_stage, w_hi, w_lo, rt_f, ct_f, cl_f, cr_f, rt_hi, rt_lo, ct2, cl_hi, cl_lo, cr_hi, cr_lo,
-    co, co_core, co_in, co_z, rg, rg_hi, rg_lo, rg_in, v_hi, v_lo,
+    co, co_core, co_in, rg, rg_hi, rg_lo, rg_in, rg_z, v_hi, v_lo,
     gram, g_core, g_first, g_second, g_third, cyw, c_core, c_first, c_second, c_third, zed, z_core, z_first, z_second, z_third,
     in_sem, send_sem, recv_sem,
 ):
     n = Net(send_sem, recv_sem)
     barrier, greetings = meet(n)
 
-    def column_block(s):
-        half = 1 - n.c if s < 4 else n.c
-        return half * 4 + n.step("x", ORDER[s % 4])
-
-    def w_copy(s):
-        return pltpu.make_async_copy(
-            window.at[:, pl.ds(pl.multiple_of(column_block(s) * 256, 256), 256)], w_stage.at[s], in_sem.at[s])
-
-    w_copies = [w_copy(s) for s in range(8)]
-    loads = [pltpu.make_async_copy(a, b, in_sem.at[8 + i]) for i, (a, b) in enumerate(
-        ((co_test, ct_f), (range_test, rt_f), (core_right, cr_f), (core_left, cl_f)))]
+    rows_of = [n.rows(n.step("y", k) * 256, 256) for k in ORDER]
+    w_copies = [pltpu.make_async_copy(window.at[rows_of[s]], w_stage.at[s], in_sem.at[s]) for s in range(4)]
+    loads = [pltpu.make_async_copy(a, b, in_sem.at[4 + i]) for i, (a, b) in enumerate(
+        ((range_test, rt_f), (co_test, ct_f), (core_right, cr_f), (core_left, cl_f)))]
     loads[0].start()
-    for c in w_copies + loads[1:]:
+    for c in w_copies[:2]:
         c.start()
 
+    def split_rows(s):
+        w_copies[s].wait()
+        w_hi[rows_of[s], :], w_lo[rows_of[s], :] = split(w_stage[s])
+
+    def range_block(s):
+        rows = rows_of[s]
+        value = mm3((w_hi[rows, :], w_lo[rows, :]), (rt_hi[...], rt_lo[...]), NN)
+        rg[rows, :] = value
+        rg_hi[rows, :], rg_lo[rows, :] = split(value)
+
     loads[0].wait()
+    rt_hi[...], rt_lo[...] = split(rt_f[...])
+    for c in w_copies[2:] + loads[1:2]:
+        c.start()
+    y_copies = []
+    for s in range(3):
+        split_rows(s)
+        range_block(s)
+        if s == 0:
+            pl.semaphore_wait(barrier, greetings)
+            loads[2].start()
+        y_copies.append(n.copy(rg.at[rows_of[s]], rg_in.at[s], n.at(y=n.step("y", ORDER[s]))))
+    loads[3].start()
+    split_rows(3)
+
+    loads[1].wait()
     ct2[0:256, :], ct2[256:512, :] = split(ct_f[...])
 
-    def co_block(s):
-        w_copies[s].wait()
-        block = column_block(s)
+    def co_block(half, k):
+        block = half * 4 + n.step("x", k)
         cols = pl.ds(pl.multiple_of(block * 256, 256), 256)
-        w_hi[:, cols], w_lo[:, cols] = split(w_stage[s])
         both = mm(ct2[...], w_hi[:, cols], NN)
         value = (both[:256] + both[256:]) + mm(ct2[0:256, :], w_lo[:, cols], NN)
         co[n.rows(block * 512, 256), :] = value[:, :128]
@@ -204,32 +220,21 @@
 
     core_copies = []
     for s in range(4):
-        at = co_block(s)
-        if s == 0:
-            pl.semaphore_wait(barrier, greetings)
+        at = co_block(1 - n.c, ORDER[s])
         core_copies.append(n.copy(co.at[at], co_core.at[s], n.partner))
     x_copies = []
+    zh_far, z_far = 1 - n.zh, n.step("z", 2)
     for s in range(4):
-        at = co_block(4 + s)
+        at = co_block(n.c, ORDER[s])
         core_copies[s].wait_recv()
         co[at, :] = co[at, :] + co_core[s]
+        x = n.step("x", ORDER[s])
+        base = (n.c * 4 + x) * 512
+        x_copies.append(n.copy(co.at[n.rows(base + zh_far * 256, 256)], co_in.at[len(x_copies)], n.at(x=x, z=z_far)))
         if ORDER[s]:
-            x_copies.append(n.copy(co.at[at], co_in.at[s], n.at(x=n.step("x", ORDER[s]))))
+            x_copies.append(n.copy(co.at[n.rows(base + n.zh * 256, 256)], co_in.at[len(x_copies)], n.at(x=x)))
     co_own = (n.c * 4 + n.x) * 512
-
-    loads[1].wait()
-    rt_hi[...], rt_lo[...] = split(rt_f[...])
-    y_copies = []
-    for s in range(4):
-        q = n.step("y", ORDER[s])
-        rows = n.rows(q * 256, 256)
-        value = mm3((w_hi[rows, :], w_lo[rows, :]), (rt_hi[...], rt_lo[...]), NN)
-        rg[rows, :] = value
-        rg_hi[rows, :], rg_lo[rows, :] = split(value)
-        for flipped in (1, 0):
-            if ORDER[s] or flipped:
-                z, zl = (n.flip, 1 - n.zl) if flipped else (n.z, n.zl)
-                y_copies.append(n.copy(rg.at[n.rows(q * 256 + zl * 128, 128)], rg_in.at[len(y_copies)], n.at(y=q, z=z)))
+    range_block(3)
 
     loads[2].wait()
     cr_hi[...], cr_lo[...] = split(cr_f[...])
@@ -239,81 +244,78 @@
         value = mm3((w_hi[rows, :], w_lo[rows, :]), (cr_hi[...], cr_lo[...]), NT)
         v_hi[rows, :], v_lo[rows, :] = split(value)
 
-    pl.loop(0, 2)(v_block)
-    total = co[n.rows(co_own, 512), :]
-    for k, c in enumerate(x_copies):
-        c.wait_recv()
-        total = total + co_in[k]
-    co[n.rows(co_own, 512), :] = total
-    zh_peer = n.at(z=n.step("z", 2))
-    co_z_copy = n.copy(co.at[n.rows(co_own + (1 - n.zh) * 256, 256)], co_z, zh_peer)
-    pl.loop(2, 4)(v_block)
-
-    y_own = n.rows(n.y * 256 + n.zl * 128, 128)
-    total = rg[y_own, :]
+    pl.loop(0, 3)(v_block)
+    y_half = rows_of[3]
+    total = rg[y_half, :]
     for k, c in enumerate(y_copies):
         c.wait_recv()
         total = total + rg_in[k]
-    y_out[y_own, :] = total
-    y_z_copy = n.copy(y_out.at[y_own], y_out.at[y_own], n.at(z=n.flip))
-    part = split(total)
-    gram[pl.ds(0, 256), :] = mm3(part, part, TN) * (1.0 / 16384)
-    w_own = n.rows(co_own + n.zh * 256, 256)
-    co_z_copy.wait_recv()
-    total = co[w_own, :] + co_z[...]
-    w_out[w_own, :] = total
-    w_z_copy = n.copy(w_out.at[w_own], w_out.at[w_own], zh_peer)
-    part = split(total)
-    gram[pl.ds(256, 256), :] = mm3(part, part, NT) * (1.0 / 16384)
-    reduce_g = Reduce(n, AXES[0], 16, gram, gram_out, g_core, g_first, g_second, g_third)
-    reduce_g.core_send()
+    rg[y_half, :] = total
+    z_flip = n.at(z=n.flip)
+    rg_z_copy = n.copy(rg.at[n.rows(n.y * 256 + (1 - n.zl) * 128, 128)], rg_z, z_flip)
+    pl.loop(3, 4)(v_block)
 
     loads[3].wait()
     cl_hi[...], cl_lo[...] = split(cl_f[...])
     left = (cl_hi[...], cl_lo[...])
+    zed[pl.ds(0, 512), :] = mm3(left, (v_hi[:, 0:256], v_lo[:, 0:256]), NN)
+    zed[pl.ds(512, 512), :] = mm3(left, (v_hi[:, 256:512], v_lo[:, 256:512]), NN)
+    reduce_z = Reduce(n, AXES[2], 32, zed, z_out, z_core, z_first, z_second, z_third)
+    reduce_z.core_send()
     cyw[pl.ds(0, 512), :] = mm3(left, (rg_hi[...], rg_lo[...]), NN)
-    reduce_g.core_done()
+    reduce_z.core_done()
     for k in range(2):
         cols = pl.ds(k * 256, 256)
         cyw[pl.ds(512 + 256 * k, 256), :] = mm3(
             (ct2[0:256, :], ct2[256:512, :]), (v_hi[:, cols], v_lo[:, cols]), NN)
     reduce_c = Reduce(n, AXES[1], 32, cyw, cyw_out, c_core, c_first, c_second, c_third)
     reduce_c.core_send()
-    for k in range(2):
-        cols = pl.ds(k * 256, 256)
-        zed[pl.ds(512 * k, 512), :] = mm3(left, (v_hi[:, cols], v_lo[:, cols]), NN)
-        if k == 0:
-            reduce_c.core_done()
-    reduce_z = Reduce(n, AXES[2], 32, zed, z_out, z_core, z_first, z_second, z_third)
-    reduce_z.core_send()
+    y_own = n.rows(n.y * 256 + n.zl * 128, 128)
+    rg_z_copy.wait_recv()
+    total = rg[y_own, :] + rg_z[...]
+    y_out[y_own, :] = total
+    part = split(total)
+    gram[pl.ds(0, 256), :] = mm3(part, part, TN) * (1.0 / 16384)
+    reduce_c.core_done()
+    w_own = n.rows(co_own + n.zh * 256, 256)
+    total = co[w_own, :]
+    for k, c in enumerate(x_copies):
+        c.wait_recv()
+        total = total + co_in[k]
+    w_out[w_own, :] = total
+    part = split(total)
+    gram[pl.ds(256, 256), :] = mm3(part, part, NT) * (1.0 / 16384)
+    reduce_g = Reduce(n, AXES[0], 16, gram, gram_out, g_core, g_first, g_second, g_third)
+    reduce_g.core_send()
+    y_z_copy = n.copy(y_out.at[y_own], y_out.at[y_own], z_flip)
+    reduce_g.core_done()
+    w_z_copy = n.copy(w_out.at[w_own], w_out.at[w_own], n.at(z=z_far))
+    reduce_z.first_done()
     reduce_g.first_done()
-    reduce_z.core_done()
+    reduce_c.first_done()
     y_z_copy.wait_recv()
-    y_half = n.rows(n.y * 256, 256)
     y_gather = [n.copy(y_out.at[y_half], y_out.at[y_half], n.at(y=n.step("y", k))) for k in (2, 1, 3)]
+    reduce_z.second_done()
+    reduce_g.second_done()
     w_z_copy.wait_recv()
-    w_half = n.rows(co_own, 512)
-    w_gather = [n.copy(w_out.at[w_half], w_out.at[w_half], n.at(x=n.step("x", k))) for k in (2, 1, 3)]
-    reduce_g.second_done()
-    reduce_c.first_done()
+    w_pair = n.rows(co_own, 512)
+    w_gather = [n.copy(w_out.at[w_pair], w_out.at[w_pair], n.at(x=n.step("x", k))) for k in (2, 1, 3)]
+    reduce_c.second_done()
+    reduce_z.third_done()
     reduce_g.third_done()
-    reduce_z.first_done()
-    reduce_c.second_done()
+    reduce_c.third_done()
+    reduce_z.second_gathered()
     reduce_g.second_gathered()
-    reduce_c.third_done()
-    reduce_z.second_done()
+    reduce_c.second_gathered()
     reduce_g.gathered()
-    reduce_c.second_gathered()
-    reduce_z.third_done()
     for c in w_gather:
         c.wait_recv()
     w_half = n.rows(n.c * 2048, 2048)
     w_core_copy = n.copy(w_out.at[w_half], w_out.at[w_half], n.partner)
-    reduce_z.second_gathered()
+    reduce_z.gathered()
     reduce_c.gathered()
     for c in y_gather:
         c.wait_recv()
-    reduce_z.gathered()
     reduce_g.core_gathered()
     w_core_copy.wait_recv()
     reduce_c.core_gathered()
@@ -333,12 +335,12 @@
         return [f(32 * r, 256), f(16 * r, 256), f(3, 4 * r, 256), f(3, r, 256), f(4, r, 256)]
 
     scratch = [
-        f(8, 1024, 256), b(1024, 2048), b(1024, 2048), f(2048, 256), f(256, 1024), f(512, 1024), f(512, 2048),
+        f(4, 256, 2048), b(1024, 2048), b(1024, 2048), f(2048, 256), f(256, 1024), f(512, 1024), f(512, 2048),
         b(2048, 256), b(2048, 256), b(512, 1024), b(512, 1024), b(512, 1024), b(512, 2048), b(512, 2048),
-        f(4096, 128), f(4, 512, 128), f(3, 512, 128), f(256, 128),
-        f(1024, 256), b(1024, 256), b(1024, 256), f(7, 128, 256), b(1024, 512), b(1024, 512),
+        f(4096, 128), f(4, 512, 128), f(7, 256, 128),
+        f(1024, 256), b(1024, 256), b(1024, 256), f(3, 256, 256), f(128, 256), b(1024, 512), b(1024, 512),
         *reduce_bufs(16), *reduce_bufs(32), *reduce_bufs(32),
-        pltpu.SemaphoreType.DMA((12,)), pltpu.SemaphoreType.DMA((COPIES,)), pltpu.SemaphoreType.DMA((COPIES,)),
+        pltpu.SemaphoreType.DMA((8,)), pltpu.SemaphoreType.DMA((COPIES,)), pltpu.SemaphoreType.DMA((COPIES,)),
     ]
     return pl.pallas_call(
         exchange_kernel,

time: 105 us -> 96.2 us (0.916)
  Pallas kernels: 104 us -> 95.2 us
    pallas_call x1, Pallas kernels: 86.4 us -> 77.4 us  [exchange(): pl.pallas_call(exchange_kernel, out_shape=[jax.ShapeDtypeStruct(s, F32) f...]
where the time goes in v4:
time: 96.2 us; the launch traced here: 96 us
  Pallas kernels  95.2 us (99%)
    pallas_call x1, Pallas kernels, exchange(): pl.pallas_call(exchange_kernel, out_shape=[jax.ShapeDtypeStruct(s, F32) f...  77.4 us
    pallas_call x1, Pallas kernels, final(): pl.pallas_call(final_kernel, out_shape=[jax.ShapeDtypeStruct(s, F32) for...  17.8 us

profile of v4, /device:TPU:1, one launch (start us, length us, event | category | flops | bytes accessed | tf_op | source)
XLA Modules:
  0.0 96.0 jit_solution(5896833288444606810)
XLA Ops:
  0.6 77.4 %exchange.1 = (f32[1024,256]{1,0:T(8,128)}, f32[4096,128]{1,0:T(8,128)}, f32[512,256]{1,0:T(8,128)}, f32[1024,256]{1,0:T(8,128)}, f32[1024,256]{1,0:T(8,128)}) custom-call(f32[1024,2048]{1,0:T(8,128)} %window.1, f32[2048,256]{1,0:T(8,128)} %range_test.1, f32[256,1024]{1,0:T(8,128)} %co_test.1, f32[512,1024]{1,0:T(8,128)} %core_left.1, f32[512,2048]{1,0:T(8,128)} %core_right.1), custom_call_target="tpu_custom_call" | custom-call | tf_op jit(solution)/shard_map/exchange/pallas_call | solution.py:345
  78.1 17.8 %final.1 = (f32[1024,256]{1,0:T(8,128)}, f32[256,2048]{1,0:T(8,128)}, f32[256,256]{1,0:T(8,128)}) custom-call(f32[1024,256]{1,0:T(8,128)} %get-tuple-element.8.y_hbm, f32[4096,128]{1,0:T(8,128)} %get-tuple-element.9.w_hbm, f32[512,256]{1,0:T(8,128)} %get-tuple-element.10.gram, f32[1024,256]{1,0:T(8,128)} %get-tuple-element.11.cyw, ...), custom_call_target="tpu_custom_call" | custom-call | tf_op jit(solution)/shard_map/final/pallas_call | solution.py:488

commit v5 on v4

--- a/solution.py
+++ b/solution.py
@@ -164,11 +164,12 @@
 
 def exchange_kernel(
     window, range_test, co_test, core_left, core_right,
+    y_hbm, w_hbm, gram_hbm, cyw_hbm, z_hbm,
     y_out, w_out, gram_out, cyw_out, z_out,
     w_stage, w_hi, w_lo, rt_f, ct_f, cl_f, cr_f, rt_hi, rt_lo, ct2, cl_hi, cl_lo, cr_hi, cr_lo,
     co, co_core, co_in, rg, rg_hi, rg_lo, rg_in, rg_z, v_hi, v_lo,
     gram, g_core, g_first, g_second, g_third, cyw, c_core, c_first, c_second, c_third, zed, z_core, z_first, z_second, z_third,
-    in_sem, send_sem, recv_sem,
+    in_sem, out_sem, send_sem, recv_sem,
 ):
     n = Net(send_sem, recv_sem)
     barrier, greetings = meet(n)
@@ -312,14 +313,27 @@
         c.wait_recv()
     w_half = n.rows(n.c * 2048, 2048)
     w_core_copy = n.copy(w_out.at[w_half], w_out.at[w_half], n.partner)
+    stores = []
+
+    def store(src, dst):
+        stores.append(pltpu.make_async_copy(src, dst, out_sem.at[len(stores)]))
+        stores[-1].start()
+
     reduce_z.gathered()
     reduce_c.gathered()
     for c in y_gather:
         c.wait_recv()
+    store(y_out, y_hbm)
     reduce_g.core_gathered()
+    store(gram_out, gram_hbm)
     w_core_copy.wait_recv()
+    store(w_out, w_hbm)
+    reduce_z.core_gathered()
+    store(z_out, z_hbm)
     reduce_c.core_gathered()
-    reduce_z.core_gathered()
+    store(cyw_out, cyw_hbm)
+    for c in stores:
+        c.wait()
     for c in n.copies:
         c.wait_send()
 
@@ -335,19 +349,20 @@
         return [f(32 * r, 256), f(16 * r, 256), f(3, 4 * r, 256), f(3, r, 256), f(4, r, 256)]
 
     scratch = [
+        f(1024, 256), f(4096, 128), f(512, 256), f(1024, 256), f(1024, 256),
         f(4, 256, 2048), b(1024, 2048), b(1024, 2048), f(2048, 256), f(256, 1024), f(512, 1024), f(512, 2048),
         b(2048, 256), b(2048, 256), b(512, 1024), b(512, 1024), b(512, 1024), b(512, 2048), b(512, 2048),
         f(4096, 128), f(4, 512, 128), f(7, 256, 128),
         f(1024, 256), b(1024, 256), b(1024, 256), f(3, 256, 256), f(128, 256), b(1024, 512), b(1024, 512),
         *reduce_bufs(16), *reduce_bufs(32), *reduce_bufs(32),
-        pltpu.SemaphoreType.DMA((8,)), pltpu.SemaphoreType.DMA((COPIES,)), pltpu.SemaphoreType.DMA((COPIES,)),
+        pltpu.SemaphoreType.DMA((8,)), pltpu.SemaphoreType.DMA((5,)), pltpu.SemaphoreType.DMA((COPIES,)), pltpu.SemaphoreType.DMA((COPIES,)),
     ]
     return pl.pallas_call(
         exchange_kernel,
         out_shape=[jax.ShapeDtypeStruct(s, F32) for s in (
             (1024, 256), (4096, 128), (512, 256), (1024, 256), (1024, 256))],
         in_specs=[pl.BlockSpec(memory_space=pl.ANY)] * 5,
-        out_specs=[pl.BlockSpec(memory_space=pltpu.VMEM)] * 5,
+        out_specs=[pl.BlockSpec(memory_space=pl.ANY)] * 5,
         scratch_shapes=scratch,
         compiler_params=pltpu.CompilerParams(collective_id=0, has_side_effects=True, vmem_limit_bytes=67043328),
         name="exchange",

time: 96.2 us -> 94.7 us (0.984)
  Pallas kernels: 95.2 us -> 93.7 us
    pallas_call x1, Pallas kernels: 77.4 us -> 76 us  [exchange(): pl.pallas_call(exchange_kernel, out_shape=[jax.ShapeDtypeStruct(s, F32) f...]
where the time goes in v5:
time: 94.7 us; the launch traced here: 94.5 us
  Pallas kernels  93.7 us (99%)
    pallas_call x1, Pallas kernels, exchange(): pl.pallas_call(exchange_kernel, out_shape=[jax.ShapeDtypeStruct(s, F32) f...  76 us
    pallas_call x1, Pallas kernels, final(): pl.pallas_call(final_kernel, out_shape=[jax.ShapeDtypeStruct(s, F32) for...  17.8 us

profile of v5, /device:TPU:1, one launch (start us, length us, event | category | flops | bytes accessed | tf_op | source)
XLA Modules:
  0.0 94.5 jit_solution(8030977429132854297)
XLA Ops:
  0.6 76.0 %exchange.1 = (f32[1024,256]{1,0:T(8,128)}, f32[4096,128]{1,0:T(8,128)}, f32[512,256]{1,0:T(8,128)}, f32[1024,256]{1,0:T(8,128)}, f32[1024,256]{1,0:T(8,128)}) custom-call(f32[1024,2048]{1,0:T(8,128)} %window.1, f32[2048,256]{1,0:T(8,128)} %range_test.1, f32[256,1024]{1,0:T(8,128)} %co_test.1, f32[512,1024]{1,0:T(8,128)} %core_left.1, f32[512,2048]{1,0:T(8,128)} %core_right.1), custom_call_target="tpu_custom_call" | custom-call | tf_op jit(solution)/shard_map/exchange/pallas_call | solution.py:360
  76.6 17.8 %final.1 = (f32[1024,256]{1,0:T(8,128)}, f32[256,2048]{1,0:T(8,128)}, f32[256,256]{1,0:T(8,128)}) custom-call(f32[1024,256]{1,0:T(8,128)} %get-tuple-element.8.y_hbm, f32[4096,128]{1,0:T(8,128)} %get-tuple-element.9.w_hbm, f32[512,256]{1,0:T(8,128)} %get-tuple-element.10.gram, f32[1024,256]{1,0:T(8,128)} %get-tuple-element.11.cyw, ...), custom_call_target="tpu_custom_call" | custom-call | tf_op jit(solution)/shard_map/final/pallas_call | solution.py:503
